TPU v7x, 512 devices: a whole 4x8x8 slice. The times are simulated.
512 devices in a mesh: energy: 32 (over z_lo, y), slab: 16 (over x, z_hi, core).
Axes of the slice: x: 4, y: 8, z: 8 (z_hi: 2, z_lo: 4; z = z_hi * 4 + z_lo), core: 2. Of those that a mesh axis runs over, the one named last changes fastest.
Arguments:
- green_blocks: bfloat16 [64, 16, 512, 512], P('energy', 'slab'), may hold values from -6 to 6
- coupling: bfloat16 [16, 512, 512], P('slab'), may hold values from -0.25 to 0.25
- coulomb: bfloat16 [16, 512, 512], P('slab'), may hold values from -0.25 to 0.25
Outputs:
- self_energy: bfloat16 [64, 16, 512, 512], P('energy', 'slab')
- screening: bfloat16 [64, 16, 512, 512], P('energy', 'slab')
All inputs are finite; a program needn't handle non-finite values.
Results may differ from a plain program's by a relative error of at most 0.0075.
Values may be sent and summed in bfloat16 or wider, within the bound.
No kernel may reach another device: no remote copies, remote signals or barrier semaphores. Data moves between devices by JAX's collectives and lax.ppermute only.
A program may use at most 64 MiB of HBM per device.

v0:
```python
import math

import jax
import jax.numpy as jnp
from jax import lax
from jax.sharding import PartitionSpec as P


def from_behind(block, axis, distance):
    devices = range(lax.axis_size(axis))
    route = [(i - distance, i) for i in devices if i - distance in devices]
    return lax.ppermute(block, axis, route)


def cut_along(array, dim, count):
    before, after = (array.shape[:dim], array.shape[dim + 1 :])
    return jnp.moveaxis(array.reshape(*before, count, -1, *after), dim, 0)


def piece_ends(length, count):
    unit = 8 if length >= 8 * count else 1
    return [length // unit * k // count * unit for k in range(1, count)]


def laid_out(parts, dim):
    parts = jnp.moveaxis(parts, 0, dim)
    dims = parts.shape
    return parts.reshape(*dims[:dim], dims[dim] * dims[dim + 1], *dims[dim + 2 :])


def cut_exchange(array, axis, pieces, split_dim, concat_dim):
    parts = cut_along(array, split_dim, lax.axis_size(axis))
    split_at = max(range(1, max(2, parts.ndim - 1)), key=lambda d: parts.shape[d])
    gathered = []
    for share in jnp.split(parts, piece_ends(parts.shape[split_at], pieces), axis=split_at):
        if share.size:
            gathered.append(lax.all_to_all(share, axis, split_axis=0, concat_axis=0, tiled=True))
    return laid_out(jnp.concatenate(gathered, axis=split_at), concat_dim)


def with_halo(array, sides, width):
    for axis, dim in sides:
        count, length = (lax.axis_size(axis), array.shape[dim])
        up = [(i, (i + 1) % count) for i in range(count - 1)]
        down = [(j, i) for i, j in up]
        last = lax.slice_in_dim(array, length - width, length, axis=dim)
        leading = lax.slice_in_dim(array, 0, width, axis=dim)
        before = lax.ppermute(last, axis, up)
        after = lax.ppermute(leading, axis, down)
        array = jnp.concatenate([before, array, after], axis=dim)
    return array


def tables(count):
    indices = jnp.arange(count, dtype=jnp.int32)
    product = indices[:, None] * indices[None, :] % count
    angles = product.astype(jnp.float32) * (2.0 * math.pi / count)
    return (jnp.cos(angles), jnp.sin(angles))


def correlate(blocks):
    count = blocks.shape[0]
    cosine, sine = tables(count)
    flattened = blocks.astype(jnp.float32).reshape(count, -1)
    cosine_part = jnp.dot(cosine, flattened, precision=lax.Precision.HIGHEST)
    sine_part = jnp.dot(sine, flattened, precision=lax.Precision.HIGHEST)
    spectrum = cosine_part * cosine_part + sine_part * sine_part
    folded = jnp.dot(cosine, spectrum, precision=lax.Precision.HIGHEST) * (
        1.0 / (count * math.sqrt(count))
    )
    return folded.reshape(blocks.shape).astype(jnp.bfloat16)


def dress_lower(blocks, link):
    inner = jnp.einsum("eij,jk->eik", blocks, link, preferred_element_type=jnp.float32).astype(
        jnp.bfloat16
    )
    return jnp.einsum("ji,ejk->eik", link, inner, preferred_element_type=jnp.float32).astype(
        jnp.bfloat16
    )


def dress_upper(blocks, link):
    inner = jnp.einsum("eij,kj->eik", blocks, link, preferred_element_type=jnp.float32).astype(
        jnp.bfloat16
    )
    return jnp.einsum("ij,ejk->eik", link, inner, preferred_element_type=jnp.float32).astype(
        jnp.bfloat16
    )


def on_device(green_blocks, coupling, coulomb):
    own_green = green_blocks[:, 0]
    own_link = coupling[0]
    link_below = from_behind(coupling, "slab", 1)[0]
    for_above = dress_lower(own_green, own_link)
    for_below = dress_upper(own_green, link_below)
    lower = from_behind(for_above, "slab", 1)
    upper = from_behind(for_below, "slab", -1)
    sigma = (lower.astype(jnp.float32) + upper.astype(jnp.float32)).astype(jnp.bfloat16)
    entry_rows = lax.all_to_all(green_blocks, "energy", split_axis=2, concat_axis=0, tiled=True)
    polar_rows = correlate(entry_rows)
    polar = cut_exchange(polar_rows, "energy", 2, 0, 2)
    polar_rim = with_halo(polar, (("slab", 1),), 1)
    beside = polar_rim[:, 0].astype(jnp.float32) + polar_rim[:, 2].astype(jnp.float32)
    screen_block = coulomb[0]
    inner = jnp.einsum(
        "eij,kj->eik", polar[:, 0], screen_block, preferred_element_type=jnp.float32
    ).astype(jnp.bfloat16)
    outer = jnp.einsum("ij,ejk->eik", screen_block, inner, preferred_element_type=jnp.float32)
    screened = (outer + 0.5 * beside).astype(jnp.bfloat16)
    return (sigma[:, None], screened[:, None])


def solution(mesh):
    placed = (P("energy", "slab", None, None), P("slab", None, None), P("slab", None, None))
    return jax.shard_map(
        on_device,
        mesh=mesh,
        in_specs=placed,
        out_specs=(P("energy", "slab", None, None), P("energy", "slab", None, None)),
        check_vma=False,
    )
```

profile of v0, /device:TPU:99, one launch (start us, length us, event | category | flops | bytes accessed | tf_op | source)
XLA Modules:
  0.0 232.6 jit_solution(4798164044232020507)
XLA Ops:
  0.6 0.0 copy-start
  0.6 2.4 %copy.44 = bf16[2,1,512,512]{3,0,1,2:T(2,128)(2,1)S(1)} copy(bf16[2,1,512,512]{3,2,1,0:T(8,128)(2,1)} %param.3) | data formatting | bytes 2097152 | tf_op args[0]
  3.0 36.4 %all_to_all.25 = bf16[2,1,512,512]{3,0,1,2:T(2,128)(2,1)S(1)} all-to-all(bf16[2,1,512,512]{3,0,1,2:T(2,128)(2,1)S(1)} %copy.44), channel_id=1, replica_groups=mesh['energy'=32,'slab'=16] {'energy'}, dimensions={2} | all-to-all | bytes 2097152 | tf_op jit(solution)/shard_map/all_to_all | solution.py:101
  39.4 0.2 copy.45
  39.6 0.1 copy.46
  39.7 0.6 copy.60
  40.3 1.1 convolution_multiply_fusion
  41.4 1.2 fusion
  42.7 2.1 fusion.1
  44.8 0.4 copy.61
  45.2 0.0 copy-start.2
  45.2 0.0 copy-start.1
  45.2 1.0 fusion.40
  46.2 21.2 %all_to_all.26 = bf16[32,2,1,8,512]{4,3,1,2,0:T(8,128)(2,1)S(1)} all-to-all(bf16[32,2,1,8,512]{4,3,1,2,0:T(8,128)(2,1)S(1)} %get-tuple-element.12), channel_id=1, replica_groups=mesh['energy'=32,'slab'=16] {'energy'}, dimensions={0} | all-to-all | bytes 1048576 | tf_op jit(solution)/shard_map/all_to_all | solution.py:37
  67.4 8.8 %all-to-all-start.2 = ((bf16[32,2,1,8,512]{4,3,1,2,0:T(8,128)(2,1)}), bf16[32,2,1,8,512]{4,3,1,2,0:T(8,128)(2,1)S(1)}, u32[]{:S(2)}, u32[]{:S(2)}) async-start(bf16[32,2,1,8,512]{4,3,1,2,0:T(8,128)(2,1)} %get-tuple-element.13), calls=%async_computation.2 | async-start | bytes 1048576 | tf_op jit(solution)/shard_map/all_to_all | solution.py:37
  76.1 0.0 copy-done.2
  76.1 9.3 %collective-permute-start.1 = (bf16[1,512,512]{2,1,0:T(8,128)(2,1)S(1)}, bf16[1,512,512]{2,1,0:T(8,128)(2,1)}, u32[]{:S(2)}, u32[]{:S(2)}) collective-permute-start(bf16[1,512,512]{2,1,0:T(8,128)(2,1)S(1)} %copy-done.2), channel_id=1, source_target_pairs={{0,1},{1,2},{2,3},{3,4},{4,5},{5,6},{6,7},{7,8},{8,9},{9,10},{10,1... | collective-permute-start | bytes 1572872 | tf_op jit(solution)/shard_map/ppermute | solution.py:12
  85.4 0.0 copy-done.1
  85.4 2.3 fusion.4
  87.7 1.9 collective-permute-start
  89.7 7.8 %collective-permute-done.1 = bf16[1,512,512]{2,1,0:T(8,128)(2,1)} collective-permute-done((bf16[1,512,512]{2,1,0:T(8,128)(2,1)S(1)}, bf16[1,512,512]{2,1,0:T(8,128)(2,1)}, u32[]{:S(2)}, u32[]{:S(2)}) %collective-permute-start.1) | collective-permute-done | bytes 524320 | tf_op jit(solution)/shard_map/ppermute | solution.py:12
  97.4 3.5 %fusion.5 = bf16[2,512,512]{1,2,0:T(8,128)(2,1)} fusion(bf16[2,1,512,512]{3,2,1,0:T(8,128)(2,1)S(1)} %copy-done.1, bf16[1,512,512]{2,1,0:T(8,128)(2,1)} %collective-permute-done.1), kind=kOutput, calls=%fused_computation.15 | convolution fusion | flops 1074790400 | bytes 2621440 | tf_op jit(solution)/shard_map/ij,ejk->eik/dot_general | solution.py:87
  100.9 4.8 %collective-permute-start.2 = (bf16[2,512,512]{1,2,0:T(8,128)(2,1)}, bf16[2,512,512]{1,2,0:T(8,128)(2,1)}, u32[]{:S(2)}, u32[]{:S(2)}) collective-permute-start(bf16[2,512,512]{1,2,0:T(8,128)(2,1)} %fusion.5), channel_id=1, source_target_pairs={{1,0},{2,1},{3,2},{4,3},{5,4},{6,5},{7,6},{8,7},{9,8},{10,9},{11,1... | collective-permute-start | bytes 3145736 | tf_op jit(solution)/shard_map/ppermute | solution.py:12
  105.7 0.0 all-to-all-done.2
  105.7 0.1 pad_maximum_fusion
  105.8 0.1 copy.59
  105.9 1.3 copy.52
  107.2 80.4 %collective-permute-start.3 = (bf16[2,1,512,512]{2,3,0,1:T(8,128)(2,1)}, bf16[2,1,512,512]{2,3,0,1:T(8,128)(2,1)}, u32[]{:S(2)}, u32[]{:S(2)}) collective-permute-start(bf16[2,1,512,512]{2,3,0,1:T(8,128)(2,1)} %copy.52), channel_id=1, source_target_pairs={{0,1},{1,2},{2,3},{3,4},{4,5},{5,6},{6,7},{7,8},{8,9},{9,10},{10,1... | collective-permute-start | bytes 3145736 | tf_op jit(solution)/shard_map/ppermute | solution.py:48
  187.7 1.9 collective-permute-start.4
  189.6 0.0 collective-permute-done
  189.6 0.0 collective-permute-done.2
  189.6 1.8 fusion.6
  191.5 1.3 copy.54
  192.8 29.4 %collective-permute-done.3 = bf16[2,1,512,512]{2,3,0,1:T(8,128)(2,1)} collective-permute-done((bf16[2,1,512,512]{2,3,0,1:T(8,128)(2,1)}, bf16[2,1,512,512]{2,3,0,1:T(8,128)(2,1)}, u32[]{:S(2)}, u32[]{:S(2)}) %collective-permute-start.3) | collective-permute-done | bytes 1048608 | tf_op jit(solution)/shard_map/ppermute | solution.py:48
  222.2 6.2 %collective-permute-done.4 = bf16[2,1,512,512]{2,3,0,1:T(8,128)(2,1)} collective-permute-done((bf16[2,1,512,512]{2,3,0,1:T(8,128)(2,1)}, bf16[2,1,512,512]{2,3,0,1:T(8,128)(2,1)}, u32[]{:S(2)}, u32[]{:S(2)}) %collective-permute-start.4) | collective-permute-done | bytes 1048608 | tf_op jit(solution)/shard_map/ppermute | solution.py:49
  228.3 0.0 copy-done
  228.3 2.9 %fusion.3 = bf16[2,1,512,512]{2,3,0,1:T(8,128)(2,1)S(1)} fusion(bf16[2,1,512,512]{2,3,0,1:T(8,128)(2,1)} %collective-permute-done.4, bf16[2,1,512,512]{2,3,0,1:T(8,128)(2,1)} %collective-permute-done.3, bf16[2,512,512]{2,1,0:T(8,128)(2,1)S(1)} %bitcast.67, bf16[1,512,512]{2,1,0:T(8,128)(2,1)S(1)} %copy-done), kind=kOutput, calls=%fused_computation.13 | convolution fusion | flops 1077411840 | bytes 4718592 | tf_op jit(solution)/shard_map/ij,ejk->eik/dot_general | solution.py:110
  231.2 1.3 copy.55
Async XLA Ops:
  0.6 227.7 %copy-start = (bf16[1,512,512]{2,1,0:T(8,128)(2,1)S(1)}, bf16[1,512,512]{2,1,0:T(8,128)(2,1)}, u32[]{:S(2)}) copy-start(bf16[1,512,512]{2,1,0:T(8,128)(2,1)} %param.5) | copy-start | bytes 1572868
  45.2 30.9 %copy-start.2 = (bf16[1,512,512]{2,1,0:T(8,128)(2,1)S(1)}, bf16[1,512,512]{2,1,0:T(8,128)(2,1)}, u32[]{:S(2)}) copy-start(bf16[1,512,512]{2,1,0:T(8,128)(2,1)} %param.4) | copy-start | bytes 1572868
  45.2 40.2 %copy-start.1 = (bf16[2,1,512,512]{3,2,1,0:T(8,128)(2,1)S(1)}, bf16[2,1,512,512]{3,2,1,0:T(8,128)(2,1)}, u32[]{:S(2)}) copy-start(bf16[2,1,512,512]{3,2,1,0:T(8,128)(2,1)} %param.3) | copy-start | bytes 3145732
  67.4 38.3 %all-to-all-start.2 = ((bf16[32,2,1,8,512]{4,3,1,2,0:T(8,128)(2,1)}), bf16[32,2,1,8,512]{4,3,1,2,0:T(8,128)(2,1)S(1)}, u32[]{:S(2)}, u32[]{:S(2)}) async-start(bf16[32,2,1,8,512]{4,3,1,2,0:T(8,128)(2,1)} %get-tuple-element.13), calls=%async_computation.2 | async-start | bytes 1048576 | tf_op jit(solution)/shard_map/all_to_all | solution.py:37
  76.1 21.3 %collective-permute-start.1 = (bf16[1,512,512]{2,1,0:T(8,128)(2,1)S(1)}, bf16[1,512,512]{2,1,0:T(8,128)(2,1)}, u32[]{:S(2)}, u32[]{:S(2)}) collective-permute-start(bf16[1,512,512]{2,1,0:T(8,128)(2,1)S(1)} %copy-done.2), channel_id=1, source_target_pairs={{0,1},{1,2},{2,3},{3,4},{4,5},{5,6},{6,7},{7,8},{8,9},{9,10},{10,1... | collective-permute-start | bytes 1572872 | tf_op jit(solution)/shard_map/ppermute | solution.py:12
  87.7 101.9 %collective-permute-start = (bf16[2,512,512]{1,2,0:T(8,128)(2,1)}, bf16[2,512,512]{1,2,0:T(8,128)(2,1)}, u32[]{:S(2)}, u32[]{:S(2)}) collective-permute-start(bf16[2,512,512]{1,2,0:T(8,128)(2,1)} %fusion.4), channel_id=1, source_target_pairs={{0,1},{1,2},{2,3},{3,4},{4,5},{5,6},{6,7},{7,8},{8,9},{9,10},{10,1... | collective-permute-start | bytes 3145736 | tf_op jit(solution)/shard_map/ppermute | solution.py:12
  100.9 88.7 %collective-permute-start.2 = (bf16[2,512,512]{1,2,0:T(8,128)(2,1)}, bf16[2,512,512]{1,2,0:T(8,128)(2,1)}, u32[]{:S(2)}, u32[]{:S(2)}) collective-permute-start(bf16[2,512,512]{1,2,0:T(8,128)(2,1)} %fusion.5), channel_id=1, source_target_pairs={{1,0},{2,1},{3,2},{4,3},{5,4},{6,5},{7,6},{8,7},{9,8},{10,9},{11,1... | collective-permute-start | bytes 3145736 | tf_op jit(solution)/shard_map/ppermute | solution.py:12
  107.2 114.9 %collective-permute-start.3 = (bf16[2,1,512,512]{2,3,0,1:T(8,128)(2,1)}, bf16[2,1,512,512]{2,3,0,1:T(8,128)(2,1)}, u32[]{:S(2)}, u32[]{:S(2)}) collective-permute-start(bf16[2,1,512,512]{2,3,0,1:T(8,128)(2,1)} %copy.52), channel_id=1, source_target_pairs={{0,1},{1,2},{2,3},{3,4},{4,5},{5,6},{6,7},{7,8},{8,9},{9,10},{10,1... | collective-permute-start | bytes 3145736 | tf_op jit(solution)/shard_map/ppermute | solution.py:48
  187.7 40.7 %collective-permute-start.4 = (bf16[2,1,512,512]{2,3,0,1:T(8,128)(2,1)}, bf16[2,1,512,512]{2,3,0,1:T(8,128)(2,1)}, u32[]{:S(2)}, u32[]{:S(2)}) collective-permute-start(bf16[2,1,512,512]{2,3,0,1:T(8,128)(2,1)} %copy.52), channel_id=1, source_target_pairs={{1,0},{2,1},{3,2},{4,3},{5,4},{6,5},{7,6},{8,7},{9,8},{10,9},{11,1... | collective-permute-start | bytes 3145736 | tf_op jit(solution)/shard_map/ppermute | solution.py:49
where the time goes:
time: 233 us
  starting transfers between devices  107 us (46%)
  blocking collectives  57.6 us (25%)
  waiting for transfers between devices  43.4 us (19%)
  matrix products  13.1 us (6%)
  local copies, waits for them, and re-layouts  8.63 us (4%)
    ppermute x1, starting transfers between devices, with_halo(): before = lax.ppermute(last, axis, up)  80.4 us
    all_to_all x1, blocking collectives, on_device(): lax.all_to_all(green_blocks, 'energy', split_axis=2, concat_axis=0, tiled...  36.4 us
    ppermute x1, waiting for transfers between devices, with_halo(): before = lax.ppermute(last, axis, up)  29.4 us
    all_to_all x1, blocking collectives, cut_exchange(): lax.all_to_all(share, axis, split_axis=0, concat_axis=0, tiled=True)  21.2 us
    ppermute x3, starting transfers between devices, from_behind(): return lax.ppermute(block, axis, route)  16 us
    all_to_all x1, starting transfers between devices, cut_exchange(): lax.all_to_all(share, axis, split_axis=0, concat_axis=0, tiled=True)  8.77 us
    ppermute x3, waiting for transfers between devices, from_behind(): return lax.ppermute(block, axis, route)  7.79 us
    ppermute x1, waiting for transfers between devices, with_halo(): after = lax.ppermute(leading, axis, down)  6.16 us
  transfers between devices with their start and end apart: 6, of which 3 were waited for; matrix products, arithmetic and copies ran while one was open for 4% of the time, Pallas kernels for 0%

commit v1 on v0

v1 whole, which is shorter than its diff:
```python
import functools
import math

import jax
import jax.numpy as jnp
from jax import lax
from jax.experimental import pallas as pl
from jax.experimental.pallas import tpu as pltpu
from jax.sharding import PartitionSpec as P

F32, BF16 = jnp.float32, jnp.bfloat16
NE, SLABS, M = 64, 16, 512
ENERGY, Z_LO, Y = 32, 4, 8
ROWS = M // ENERGY
BOTH = ("energy", "slab")


def at(energy, slab):
    return energy * SLABS + slab


def along_slabs(block, step):
    route = [(s, s + step) for s in range(SLABS) if 0 <= s + step < SLABS]
    return lax.ppermute(block, "slab", route)


def home_and_across(rows):
    groups = [
        [at(e, s % SLABS) for s in (first, first + 1) for e in range(ENERGY)]
        for first in range(1, SLABS, 2)
    ]
    both = jnp.concatenate([rows, rows], axis=0)
    got = lax.all_to_all(both, BOTH, 0, 0, axis_index_groups=groups, tiled=True)
    return got.reshape(2, *rows.shape)


def on_chip(block):
    return lax.ppermute(block, "slab", [(s, s ^ 1) for s in range(SLABS)])


def dot(a, b, ca, cb):
    return lax.dot_general(a, b, (((ca,), (cb,)), ((), ())), preferred_element_type=F32)


def by_rows(green):
    return jnp.swapaxes(green.reshape(2, ENERGY, ROWS, M), 0, 1)


def lower_kernel(g_ref, h_ref, o_ref):
    inner = dot(g_ref[0], h_ref[...], 1, 0).astype(BF16)
    o_ref[0] = dot(h_ref[...], inner, 0, 0).astype(BF16)


def dress_lower(green, link):
    return pl.pallas_call(
        lower_kernel,
        out_shape=jax.ShapeDtypeStruct((2, M, M), BF16),
        grid=(2,),
        in_specs=[
            pl.BlockSpec((1, M, M), lambda e: (e, 0, 0)),
            pl.BlockSpec((M, M), lambda e: (0, 0)),
        ],
        out_specs=pl.BlockSpec((1, M, M), lambda e: (e, 0, 0)),
        cost_estimate=pl.CostEstimate(
            flops=8 * M**3, bytes_accessed=5 << 19, transcendentals=0
        ),
    )(green, link)


def sigma_kernel(g_ref, h_ref, l_ref, o_ref):
    inner = dot(g_ref[0], h_ref[...], 1, 1).astype(BF16)
    upper = dot(h_ref[...], inner, 1, 0).astype(BF16)
    o_ref[0] = (l_ref[0].astype(F32) + upper.astype(F32)).astype(BF16)


def dress_upper_and_add(green_above, link, lower):
    block = pl.BlockSpec((1, M, M), lambda e: (e, 0, 0))
    return pl.pallas_call(
        sigma_kernel,
        out_shape=jax.ShapeDtypeStruct((2, M, M), BF16),
        grid=(2,),
        in_specs=[block, pl.BlockSpec((M, M), lambda e: (0, 0)), block],
        out_specs=block,
        cost_estimate=pl.CostEstimate(
            flops=8 * M**3, bytes_accessed=7 << 19, transcendentals=0
        ),
    )(green_above, link, lower)


def screen_kernel(where, p_ref, b_ref, c_ref, o_ref):
    polar = p_ref[...].reshape(M, M)
    inner = dot(polar, c_ref[...], 1, 1).astype(BF16)
    outer = dot(c_ref[...], inner, 1, 0)
    across = b_ref[...].reshape(M, M).astype(F32)
    o_ref[...] = outer + jnp.where(where[1] > 0, 0.5 * across, 0.0)


def screen(where, got, block):
    return pl.pallas_call(
        screen_kernel,
        out_shape=jax.ShapeDtypeStruct((2, M, M), F32),
        grid_spec=pltpu.PrefetchScalarGridSpec(
            num_scalar_prefetch=1,
            grid=(2,),
            in_specs=[
                pl.BlockSpec((None, ENERGY, None, ROWS, M), lambda w, f: (f[0], 0, w, 0, 0)),
                pl.BlockSpec((None, ENERGY, None, ROWS, M), lambda w, f: (1 - f[0], 0, w, 0, 0)),
                pl.BlockSpec((M, M), lambda w, f: (0, 0)),
            ],
            out_specs=pl.BlockSpec((None, M, M), lambda w, f: (w, 0, 0)),
        ),
        cost_estimate=pl.CostEstimate(flops=8 * M**3, bytes_accessed=9 << 19, transcendentals=0),
    )(where, got, got, block)


def finish_kernel(s_ref, p_ref, o_ref):
    beside = p_ref[...].reshape(M, M).astype(F32)
    o_ref[...] = (s_ref[...] + 0.5 * beside).astype(BF16)


def finish(screened, partner):
    return pl.pallas_call(
        finish_kernel,
        out_shape=jax.ShapeDtypeStruct((2, M, M), BF16),
        grid=(2,),
        in_specs=[
            pl.BlockSpec((None, M, M), lambda w: (w, 0, 0)),
            pl.BlockSpec((ENERGY, None, ROWS, M), lambda w: (0, w, 0, 0)),
        ],
        out_specs=pl.BlockSpec((None, M, M), lambda w: (w, 0, 0)),
        cost_estimate=pl.CostEstimate(flops=4 * M**2, bytes_accessed=4 << 20, transcendentals=0),
    )(screened, partner)


def tables(count):
    indices = jnp.arange(count, dtype=jnp.int32)
    product = indices[:, None] * indices[None, :] % count
    angles = product.astype(F32) * (2.0 * math.pi / count)
    return (jnp.cos(angles), jnp.sin(angles))


def correlate(rows):
    cosine, sine = tables(NE)
    flat = rows.astype(F32).reshape(NE, -1)
    cosine_part = jnp.dot(cosine, flat, precision=lax.Precision.HIGHEST)
    sine_part = jnp.dot(sine, flat, precision=lax.Precision.HIGHEST)
    spectrum = cosine_part * cosine_part + sine_part * sine_part
    folded = jnp.dot(cosine, spectrum, precision=lax.Precision.HIGHEST) * (
        1.0 / (NE * math.sqrt(NE))
    )
    return folded.reshape(rows.shape).astype(BF16)


def on_device(green_blocks, coupling, coulomb):
    green, link, block = green_blocks[:, 0], coupling[0], coulomb[0]
    slab = lax.axis_index("slab")
    own = 1 - (slab & 1)
    across = jnp.where((slab > 0) & (slab < SLABS - 1), 1, 0)
    where = jnp.stack([own, across]).astype(jnp.int32)

    rows = lax.all_to_all(by_rows(green), "energy", 0, 0, tiled=True)
    green_above = along_slabs(green, -1)
    lower = along_slabs(dress_lower(green, link), 1)
    polar_rows = correlate(rows.reshape(NE, ROWS, M))
    polar_rows, lower = lax.optimization_barrier((polar_rows, lower))
    got = home_and_across(polar_rows.reshape(ENERGY, 2, ROWS, M))
    partner = on_chip(lax.dynamic_index_in_dim(got, own, 0, False))
    screened = finish(screen(where, got, block), partner)
    sigma = dress_upper_and_add(green_above, link, lower)
    return (sigma[:, None], screened[:, None])


def solution(mesh):
    placed = (P("energy", "slab", None, None), P("slab", None, None), P("slab", None, None))
    return jax.shard_map(
        on_device,
        mesh=mesh,
        in_specs=placed,
        out_specs=(P("energy", "slab", None, None), P("energy", "slab", None, None)),
        check_vma=False,
    )
```

time: 233 us -> 167 us (0.72)
  the two profiles are of different devices: /device:TPU:99 before, /device:TPU:1 now
where the time goes in v1:
time: 167 us; the launch traced here: 166 us
  waiting for transfers between devices  76.5 us (46%)
  starting transfers between devices  64.1 us (38%)
  Pallas kernels  14.9 us (9%)
  matrix products  4.47 us (3%)
  local copies, waits for them, and re-layouts  3.37 us (2%)
  other arithmetic  2.31 us (1%)
    all_to_all x1, waiting for transfers between devices, home_and_across(): got = lax.all_to_all(both, BOTH, 0, 0, axis_index_groups=groups, tiled=True)  46.8 us
    all_to_all x1, starting transfers between devices, home_and_across(): got = lax.all_to_all(both, BOTH, 0, 0, axis_index_groups=groups, tiled=True)  18.4 us
    ppermute x1, starting transfers between devices, on_chip(): return lax.ppermute(block, 'slab', [(s, s ^ 1) for s in range(SLABS)])  17.7 us
    all_to_all x1, waiting for transfers between devices, on_device(): rows = lax.all_to_all(by_rows(green), 'energy', 0, 0, tiled=True)  16.6 us
    ppermute x2, starting transfers between devices, along_slabs(): return lax.ppermute(block, 'slab', route)  14.5 us
    all_to_all x1, starting transfers between devices, on_device(): rows = lax.all_to_all(by_rows(green), 'energy', 0, 0, tiled=True)  13.5 us
    ppermute x2, waiting for transfers between devices, along_slabs(): return lax.ppermute(block, 'slab', route)  13.1 us
    pallas_call x1, Pallas kernels, screen(): pl.pallas_call(screen_kernel, out_shape=jax.ShapeDtypeStruct((2, M, M), F...  4.7 us
  transfers between devices with their start and end apart: 5, of which 3 were waited for; matrix products, arithmetic and copies ran while one was open for 4% of the time, Pallas kernels for 7%

profile of v1, /device:TPU:1, one launch (start us, length us, event | category | flops | bytes accessed | tf_op | source)
XLA Modules:
  0.0 166.3 jit_solution(6277789794711017228)
XLA Ops:
  0.6 2.3 %copy.13 = bf16[2,32,16,512]{3,2,0,1:T(8,128)(2,1)} copy(bf16[2,32,16,512]{3,2,1,0:T(8,128)(2,1)} %bitcast.2) | data formatting | bytes 2097152 | tf_op jit(solution)/shard_map/reshape;squeeze | solution.py:46
  2.9 13.5 %all-to-all-start = ((bf16[32,2,16,512]{3,2,1,0:T(8,128)(2,1)}), bf16[32,2,16,512]{3,2,1,0:T(8,128)(2,1)S(1)}, u32[]{:S(2)}, u32[]{:S(2)}) async-start(bf16[32,2,16,512]{3,2,1,0:T(8,128)(2,1)} %bitcast.26), calls=%async_computation | async-start | bytes 2097152 | tf_op jit(solution)/shard_map/all_to_all | solution.py:161
  16.4 3.6 %shard_map.50 = bf16[2,512,512]{2,1,0:T(8,128)(2,1)} custom-call(bf16[2,512,512]{2,1,0:T(8,128)(2,1)} %bitcast.g_ref, bf16[512,512]{1,0:T(8,128)(2,1)} %bitcast.37), custom_call_target="tpu_custom_call" | custom-call | flops 1073741824 | bytes 2621440 | tf_op jit(solution)/shard_map/pallas_call | solution.py:55
  20.0 8.8 %collective-permute-start.1 = (bf16[2,512,512]{2,1,0:T(8,128)(2,1)}, bf16[2,512,512]{2,1,0:T(8,128)(2,1)S(1)}, u32[]{:S(2)}, u32[]{:S(2)}) collective-permute-start(bf16[2,512,512]{2,1,0:T(8,128)(2,1)} %shard_map.50), channel_id=1, source_target_pairs={{0,1},{1,2},{2,3},{3,4},{4,5},{5,6},{6,7},{7,8},{8,9},{9,10},{10,1... | collective-permute-start | bytes 3145736 | tf_op jit(solution)/shard_map/ppermute | solution.py:24
  28.8 16.6 %all-to-all-done = bf16[32,2,16,512]{3,2,1,0:T(8,128)(2,1)S(1)} async-done(((bf16[32,2,16,512]{3,2,1,0:T(8,128)(2,1)}), bf16[32,2,16,512]{3,2,1,0:T(8,128)(2,1)S(1)}, u32[]{:S(2)}, u32[]{:S(2)}) %all-to-all-start) | async-done | bytes 1048608 | tf_op jit(solution)/shard_map/all_to_all | solution.py:161
  45.4 0.6 copy.10
  46.0 1.1 convolution_multiply_fusion
  47.1 1.3 fusion
  48.4 2.1 %fusion.1 = bf16[64,8192]{1,0:T(8,128)(2,1)S(1)} fusion(f32[64,8192]{1,0:T(8,128)S(1)} %fusion), kind=kOutput, calls=%fused_computation.4 | convolution fusion | flops 403759104 | bytes 3145728 | tf_op jit(solution)/shard_map/dot_general | solution.py:148
  50.5 0.4 copy.11
  50.9 13.1 %collective-permute-done.1.l_ref = bf16[2,512,512]{2,1,0:T(8,128)(2,1)S(1)} collective-permute-done((bf16[2,512,512]{2,1,0:T(8,128)(2,1)}, bf16[2,512,512]{2,1,0:T(8,128)(2,1)S(1)}, u32[]{:S(2)}, u32[]{:S(2)}) %collective-permute-start.1) | collective-permute-done | bytes 1048608 | tf_op jit(solution)/shard_map/ppermute | solution.py:24
  63.9 0.0 copy-start.1
  63.9 1.6 pad_maximum_fusion
  65.6 0.0 copy-done.1
  65.6 18.4 %all-to-all-start.1 = ((bf16[64,2,16,512]{3,2,1,0:T(8,128)(2,1)}), bf16[64,2,16,512]{3,2,1,0:T(8,128)(2,1)S(1)}, u32[]{:S(2)}, u32[]{:S(2)}) async-start(bf16[64,2,16,512]{3,2,1,0:T(8,128)(2,1)} %pad_maximum_fusion), calls=%async_computation.1 | async-start | bytes 4194304 | tf_op jit(solution)/shard_map/all_to_all | solution.py:33
  84.0 5.8 %collective-permute-start = (bf16[2,512,512]{2,1,0:T(8,128)(2,1)}, bf16[2,512,512]{2,1,0:T(8,128)(2,1)}, u32[]{:S(2)}, u32[]{:S(2)}) collective-permute-start(bf16[2,512,512]{2,1,0:T(8,128)(2,1)} %bitcast.g_ref), channel_id=1, source_target_pairs={{1,0},{2,1},{3,2},{4,3},{5,4},{6,5},{7,6},{8,7},{9,8},{10,9},{11,1... | collective-permute-start | bytes 3145736 | tf_op jit(solution)/shard_map/ppermute | solution.py:24
  89.8 46.8 %all-to-all-done.1 = bf16[64,2,16,512]{3,2,1,0:T(8,128)(2,1)S(1)} async-done(((bf16[64,2,16,512]{3,2,1,0:T(8,128)(2,1)}), bf16[64,2,16,512]{3,2,1,0:T(8,128)(2,1)S(1)}, u32[]{:S(2)}, u32[]{:S(2)}) %all-to-all-start.1) | async-done | bytes 2097184 | tf_op jit(solution)/shard_map/all_to_all | solution.py:33
  136.6 0.0 copy-start
  136.6 0.1 dynamic-slice_bitcast_fusion
  136.7 17.7 %collective-permute-start.2 = (bf16[32,2,16,512]{3,2,1,0:T(8,128)(2,1)S(1)}, bf16[32,2,16,512]{3,2,1,0:T(8,128)(2,1)}, u32[]{:S(2)}, u32[]{:S(2)}) collective-permute-start(bf16[32,2,16,512]{3,2,1,0:T(8,128)(2,1)S(1)} %dynamic-slice_bitcast_fusion), channel_id=1, source_target_pairs={{0,1},{1,0},{2,3},{3,2},{4,5},{5,4},{6,7},{7,6},{8,9},{9,8},{10,11... | collective-permute-start | bytes 3145736 | tf_op jit(solution)/shard_map/ppermute | solution.py:38
  154.4 0.7 pad_add_fusion.where
  155.0 0.0 collective-permute-done.g_ref
  155.0 3.8 %shard_map.51 = bf16[2,512,512]{2,1,0:T(8,128)(2,1)} custom-call(bf16[2,512,512]{2,1,0:T(8,128)(2,1)} %collective-permute-done.g_ref, bf16[512,512]{1,0:T(8,128)(2,1)} %bitcast.38, bf16[2,512,512]{2,1,0:T(8,128)(2,1)} %copy-done.1), custom_call_target="tpu_custom_call" | custom-call | flops 1073741824 | bytes 3670016 | tf_op jit(solution)/shard_map/pallas_call | solution.py:78
  158.9 0.0 copy-done
  158.9 4.7 %shard_map.52.s_ref = f32[2,512,512]{2,1,0:T(8,128)} custom-call(s32[2]{0:T(128)} %pad_add_fusion.where, bf16[2,32,2,16,512]{4,3,2,1,0:T(8,128)(2,1)} %bitcast.28, bf16[2,32,2,16,512]{4,3,2,1,0:T(8,128)(2,1)} %bitcast.29, bf16[512,512]{1,0:T(8,128)(2,1)} %bitcast.36), custom_call_target="tpu_custom_call" | custom-call | flops 1073741824 | bytes 4718592 | tf_op jit(solution)/shard_map/pallas_call | solution.py:99
  163.5 0.0 collective-permute-done.2.p_ref
  163.6 2.8 %shard_map.53 = bf16[2,512,512]{2,1,0:T(8,128)(2,1)} custom-call(f32[2,512,512]{2,1,0:T(8,128)} %shard_map.52.s_ref, bf16[32,2,16,512]{3,2,1,0:T(8,128)(2,1)} %collective-permute-done.2.p_ref), custom_call_target="tpu_custom_call" | custom-call | flops 1048576 | bytes 4194304 | tf_op jit(solution)/shard_map/pallas_call | solution.py:122
Async XLA Ops:
  2.9 42.5 %all-to-all-start = ((bf16[32,2,16,512]{3,2,1,0:T(8,128)(2,1)}), bf16[32,2,16,512]{3,2,1,0:T(8,128)(2,1)S(1)}, u32[]{:S(2)}, u32[]{:S(2)}) async-start(bf16[32,2,16,512]{3,2,1,0:T(8,128)(2,1)} %bitcast.26), calls=%async_computation | async-start | bytes 2097152 | tf_op jit(solution)/shard_map/all_to_all | solution.py:161
  20.0 43.9 %collective-permute-start.1 = (bf16[2,512,512]{2,1,0:T(8,128)(2,1)}, bf16[2,512,512]{2,1,0:T(8,128)(2,1)S(1)}, u32[]{:S(2)}, u32[]{:S(2)}) collective-permute-start(bf16[2,512,512]{2,1,0:T(8,128)(2,1)} %shard_map.50), channel_id=1, source_target_pairs={{0,1},{1,2},{2,3},{3,4},{4,5},{5,6},{6,7},{7,8},{8,9},{9,10},{10,1... | collective-permute-start | bytes 3145736 | tf_op jit(solution)/shard_map/ppermute | solution.py:24
  63.9 1.7 copy-start.1
  65.6 71.0 %all-to-all-start.1 = ((bf16[64,2,16,512]{3,2,1,0:T(8,128)(2,1)}), bf16[64,2,16,512]{3,2,1,0:T(8,128)(2,1)S(1)}, u32[]{:S(2)}, u32[]{:S(2)}) async-start(bf16[64,2,16,512]{3,2,1,0:T(8,128)(2,1)} %pad_maximum_fusion), calls=%async_computation.1 | async-start | bytes 4194304 | tf_op jit(solution)/shard_map/all_to_all | solution.py:33
  84.0 71.1 %collective-permute-start = (bf16[2,512,512]{2,1,0:T(8,128)(2,1)}, bf16[2,512,512]{2,1,0:T(8,128)(2,1)}, u32[]{:S(2)}, u32[]{:S(2)}) collective-permute-start(bf16[2,512,512]{2,1,0:T(8,128)(2,1)} %bitcast.g_ref), channel_id=1, source_target_pairs={{1,0},{2,1},{3,2},{4,3},{5,4},{6,5},{7,6},{8,7},{9,8},{10,9},{11,1... | collective-permute-start | bytes 3145736 | tf_op jit(solution)/shard_map/ppermute | solution.py:24
  136.6 22.3 %copy-start = (bf16[64,2,16,512]{3,2,1,0:T(8,128)(2,1)}, bf16[64,2,16,512]{3,2,1,0:T(8,128)(2,1)S(1)}, u32[]{:S(2)}) copy-start(bf16[64,2,16,512]{3,2,1,0:T(8,128)(2,1)S(1)} %all-to-all-done.1) | copy-start | bytes 6291460
  136.7 26.9 %collective-permute-start.2 = (bf16[32,2,16,512]{3,2,1,0:T(8,128)(2,1)S(1)}, bf16[32,2,16,512]{3,2,1,0:T(8,128)(2,1)}, u32[]{:S(2)}, u32[]{:S(2)}) collective-permute-start(bf16[32,2,16,512]{3,2,1,0:T(8,128)(2,1)S(1)} %dynamic-slice_bitcast_fusion), channel_id=1, source_target_pairs={{0,1},{1,0},{2,3},{3,2},{4,5},{5,4},{6,7},{7,6},{8,9},{9,8},{10,11... | collective-permute-start | bytes 3145736 | tf_op jit(solution)/shard_map/ppermute | solution.py:38

commit v2 on v1

--- a/solution.py
+++ b/solution.py
@@ -13,6 +13,7 @@
 ENERGY, Z_LO, Y = 32, 4, 8
 ROWS = M // ENERGY
 BOTH = ("energy", "slab")
+WIDE = 1000 * M**3
 
 
 def at(energy, slab):
@@ -61,30 +62,46 @@
             pl.BlockSpec((M, M), lambda e: (0, 0)),
         ],
         out_specs=pl.BlockSpec((1, M, M), lambda e: (e, 0, 0)),
+        compiler_params=pltpu.CompilerParams(vmem_limit_bytes=16 << 20),
         cost_estimate=pl.CostEstimate(
             flops=8 * M**3, bytes_accessed=5 << 19, transcendentals=0
         ),
     )(green, link)
 
 
-def sigma_kernel(g_ref, h_ref, l_ref, o_ref):
+def upper_kernel(g_ref, h_ref, o_ref):
     inner = dot(g_ref[0], h_ref[...], 1, 1).astype(BF16)
-    upper = dot(h_ref[...], inner, 1, 0).astype(BF16)
-    o_ref[0] = (l_ref[0].astype(F32) + upper.astype(F32)).astype(BF16)
-
-
-def dress_upper_and_add(green_above, link, lower):
+    o_ref[0] = dot(h_ref[...], inner, 1, 0).astype(BF16)
+
+
+def dress_upper(green_above, link):
     block = pl.BlockSpec((1, M, M), lambda e: (e, 0, 0))
     return pl.pallas_call(
-        sigma_kernel,
-        out_shape=jax.ShapeDtypeStruct((2, M, M), BF16),
-        grid=(2,),
-        in_specs=[block, pl.BlockSpec((M, M), lambda e: (0, 0)), block],
+        upper_kernel,
+        out_shape=jax.ShapeDtypeStruct((2, M, M), BF16),
+        grid=(2,),
+        in_specs=[block, pl.BlockSpec((M, M), lambda e: (0, 0))],
         out_specs=block,
-        cost_estimate=pl.CostEstimate(
-            flops=8 * M**3, bytes_accessed=7 << 19, transcendentals=0
-        ),
-    )(green_above, link, lower)
+        compiler_params=pltpu.CompilerParams(vmem_limit_bytes=16 << 20),
+        cost_estimate=pl.CostEstimate(flops=WIDE, bytes_accessed=5 << 19, transcendentals=0),
+    )(green_above, link)
+
+
+def sum_kernel(a_ref, b_ref, o_ref):
+    o_ref[...] = (a_ref[...].astype(F32) + b_ref[...].astype(F32)).astype(BF16)
+
+
+def added(a, b):
+    block = pl.BlockSpec((1, M, M), lambda e: (e, 0, 0))
+    return pl.pallas_call(
+        sum_kernel,
+        out_shape=jax.ShapeDtypeStruct((2, M, M), BF16),
+        grid=(2,),
+        in_specs=[block, block],
+        out_specs=block,
+        compiler_params=pltpu.CompilerParams(vmem_limit_bytes=16 << 20),
+        cost_estimate=pl.CostEstimate(flops=WIDE, bytes_accessed=3 << 20, transcendentals=0),
+    )(a, b)
 
 
 def screen_kernel(where, p_ref, b_ref, c_ref, o_ref):
@@ -109,6 +126,7 @@
             ],
             out_specs=pl.BlockSpec((None, M, M), lambda w, f: (w, 0, 0)),
         ),
+        compiler_params=pltpu.CompilerParams(vmem_limit_bytes=16 << 20),
         cost_estimate=pl.CostEstimate(flops=8 * M**3, bytes_accessed=9 << 19, transcendentals=0),
     )(where, got, got, block)
 
@@ -128,6 +146,7 @@
             pl.BlockSpec((ENERGY, None, ROWS, M), lambda w: (0, w, 0, 0)),
         ],
         out_specs=pl.BlockSpec((None, M, M), lambda w: (w, 0, 0)),
+        compiler_params=pltpu.CompilerParams(vmem_limit_bytes=16 << 20),
         cost_estimate=pl.CostEstimate(flops=4 * M**2, bytes_accessed=4 << 20, transcendentals=0),
     )(screened, partner)
 
@@ -158,15 +177,18 @@
     across = jnp.where((slab > 0) & (slab < SLABS - 1), 1, 0)
     where = jnp.stack([own, across]).astype(jnp.int32)
 
+    green_above = along_slabs(green, -1)
     rows = lax.all_to_all(by_rows(green), "energy", 0, 0, tiled=True)
-    green_above = along_slabs(green, -1)
-    lower = along_slabs(dress_lower(green, link), 1)
+    rows, lower_here, upper, where = lax.optimization_barrier(
+        (rows, dress_lower(green, link), dress_upper(green_above, link), where)
+    )
+    lower = along_slabs(lower_here, 1)
     polar_rows = correlate(rows.reshape(NE, ROWS, M))
-    polar_rows, lower = lax.optimization_barrier((polar_rows, lower))
     got = home_and_across(polar_rows.reshape(ENERGY, 2, ROWS, M))
+    sigma = added(lower, upper)
+    got, sigma = lax.optimization_barrier((got, sigma))
     partner = on_chip(lax.dynamic_index_in_dim(got, own, 0, False))
     screened = finish(screen(where, got, block), partner)
-    sigma = dress_upper_and_add(green_above, link, lower)
     return (sigma[:, None], screened[:, None])
 
 

time: 167 us -> 151 us (0.904)
  the two profiles are of different devices: /device:TPU:1 before, /device:TPU:35 now
where the time goes in v2:
time: 151 us
  waiting for transfers between devices  87.6 us (58%)
  starting transfers between devices  39.8 us (26%)
  Pallas kernels  9.75 us (6%)
  local copies, waits for them, and re-layouts  6.9 us (5%)
  matrix products  4.46 us (3%)
  other arithmetic  1.59 us (1%)
    ppermute x2, waiting for transfers between devices, along_slabs(): return lax.ppermute(block, 'slab', route)  55.7 us
    all_to_all x1, waiting for transfers between devices, on_device(): rows = lax.all_to_all(by_rows(green), 'energy', 0, 0, tiled=True)  31.3 us
    all_to_all x1, starting transfers between devices, on_device(): rows = lax.all_to_all(by_rows(green), 'energy', 0, 0, tiled=True)  12.3 us
    all_to_all x1, starting transfers between devices, home_and_across(): got = lax.all_to_all(both, BOTH, 0, 0, axis_index_groups=groups, tiled=True)  9.93 us
    ppermute x1, starting transfers between devices, on_chip(): return lax.ppermute(block, 'slab', [(s, s ^ 1) for s in range(SLABS)])  9.43 us
    ppermute x2, starting transfers between devices, along_slabs(): return lax.ppermute(block, 'slab', route)  8.19 us
    unnamed x12, local copies, waits for them, and re-layouts  4.39 us
  transfers between devices with their start and end apart: 5, of which 4 were waited for; matrix products, arithmetic and copies ran while one was open for 6% of the time, Pallas kernels for 6%

profile of v2, /device:TPU:35, one launch (start us, length us, event | category | flops | bytes accessed | tf_op | source)
XLA Modules:
  0.0 150.9 jit_solution(7354330263453802480)
XLA Ops:
  0.6 2.6 %collective-permute-start = (bf16[2,512,512]{2,1,0:T(8,128)(2,1)}, bf16[2,512,512]{2,1,0:T(8,128)(2,1)S(1)}, u32[]{:S(2)}, u32[]{:S(2)}) collective-permute-start(bf16[2,512,512]{2,1,0:T(8,128)(2,1)} %bitcast.30), channel_id=1, source_target_pairs={{1,0},{2,1},{3,2},{4,3},{5,4},{6,5},{7,6},{8,7},{9,8},{10,9},{11,1... | collective-permute-start | bytes 3145736 | tf_op jit(solution)/shard_map/ppermute | solution.py:25
  3.2 0.0 copy-start
  3.2 0.0 copy-start.2
  3.2 2.4 %copy.13 = bf16[2,32,16,512]{3,2,0,1:T(8,128)(2,1)} copy(bf16[2,32,16,512]{3,2,1,0:T(8,128)(2,1)} %bitcast.31) | data formatting | bytes 2097152 | tf_op jit(solution)/shard_map/reshape;squeeze | solution.py:47
  5.7 12.3 %all-to-all-start = ((bf16[32,2,16,512]{3,2,1,0:T(8,128)(2,1)}), bf16[32,2,16,512]{3,2,1,0:T(8,128)(2,1)}, u32[]{:S(2)}, u32[]{:S(2)}) async-start(bf16[32,2,16,512]{3,2,1,0:T(8,128)(2,1)} %bitcast.40), calls=%async_computation | async-start | bytes 2097152 | tf_op jit(solution)/shard_map/all_to_all | solution.py:181
  18.0 0.0 copy-done
  18.0 0.0 copy-done.2
  18.0 2.4 %shard_map.50 = bf16[2,512,512]{2,1,0:T(8,128)(2,1)} custom-call(bf16[2,512,512]{2,1,0:T(8,128)(2,1)S(1)} %bitcast.32, bf16[512,512]{1,0:T(8,128)(2,1)S(1)} %bitcast.34), custom_call_target="tpu_custom_call" | custom-call | flops 1073741824 | bytes 2621440 | tf_op jit(solution)/shard_map/pallas_call | solution.py:56
  20.4 0.1 pad_add_fusion.where
  20.5 4.2 %collective-permute-done.g_ref = bf16[2,512,512]{2,1,0:T(8,128)(2,1)S(1)} collective-permute-done((bf16[2,512,512]{2,1,0:T(8,128)(2,1)}, bf16[2,512,512]{2,1,0:T(8,128)(2,1)S(1)}, u32[]{:S(2)}, u32[]{:S(2)}) %collective-permute-start) | collective-permute-done | bytes 1048608 | tf_op jit(solution)/shard_map/ppermute | solution.py:25
  24.7 1.6 %shard_map.51.b_ref = bf16[2,512,512]{2,1,0:T(8,128)(2,1)S(1)} custom-call(bf16[2,512,512]{2,1,0:T(8,128)(2,1)S(1)} %collective-permute-done.g_ref, bf16[512,512]{1,0:T(8,128)(2,1)S(1)} %bitcast.35), custom_call_target="tpu_custom_call" | custom-call | flops 134217728000 | bytes 2621440 | tf_op jit(solution)/shard_map/pallas_call | solution.py:79
  26.4 0.0 copy-start.3
  26.4 1.0 copy-done.3
  27.3 31.3 %all-to-all-done = bf16[32,2,16,512]{3,2,1,0:T(8,128)(2,1)} async-done(((bf16[32,2,16,512]{3,2,1,0:T(8,128)(2,1)}), bf16[32,2,16,512]{3,2,1,0:T(8,128)(2,1)}, u32[]{:S(2)}, u32[]{:S(2)}) %all-to-all-start) | async-done | bytes 1048608 | tf_op jit(solution)/shard_map/all_to_all | solution.py:181
  58.6 1.8 %copy.10 = bf16[8,8,16,512]{3,1,2,0:T(8,128)(2,1)S(1)} copy(bf16[8,8,16,512]{3,2,1,0:T(8,128)(2,1)} %bitcast.16) | data formatting | bytes 2097152
  60.4 5.6 %collective-permute-start.1 = (bf16[2,512,512]{2,1,0:T(8,128)(2,1)}, bf16[2,512,512]{2,1,0:T(8,128)(2,1)}, u32[]{:S(2)}, u32[]{:S(2)}) collective-permute-start(bf16[2,512,512]{2,1,0:T(8,128)(2,1)} %shard_map.50), channel_id=1, source_target_pairs={{0,1},{1,2},{2,3},{3,4},{4,5},{5,6},{6,7},{7,8},{8,9},{9,10},{10,1... | collective-permute-start | bytes 3145736 | tf_op jit(solution)/shard_map/ppermute | solution.py:25
  66.1 1.1 convolution_multiply_fusion
  67.2 1.2 fusion
  68.4 2.1 %fusion.1 = bf16[64,8192]{1,0:T(8,128)(2,1)S(1)} fusion(f32[64,8192]{1,0:T(8,128)S(1)} %fusion), kind=kOutput, calls=%fused_computation.4 | convolution fusion | flops 403759104 | bytes 3145728 | tf_op jit(solution)/shard_map/dot_general | solution.py:167
  70.5 0.4 copy.11
  70.9 1.5 %pad_maximum_fusion = bf16[64,2,16,512]{3,2,1,0:T(8,128)(2,1)} fusion(bf16[32,2,16,512]{3,2,1,0:T(8,128)(2,1)S(1)} %bitcast.39), kind=kLoop, calls=%fused_computation.5 | loop fusion | flops 1048576 | bytes 3145728 | tf_op jit(solution)/shard_map/concatenate | solution.py:33
  72.4 9.9 %all-to-all-start.1 = ((bf16[64,2,16,512]{3,2,1,0:T(8,128)(2,1)}), bf16[64,2,16,512]{3,2,1,0:T(8,128)(2,1)S(1)}, u32[]{:S(2)}, u32[]{:S(2)}) async-start(bf16[64,2,16,512]{3,2,1,0:T(8,128)(2,1)} %pad_maximum_fusion), calls=%async_computation.1 | async-start | bytes 4194304 | tf_op jit(solution)/shard_map/all_to_all | solution.py:34
  82.4 51.5 %collective-permute-done.1.a_ref = bf16[2,512,512]{2,1,0:T(8,128)(2,1)} collective-permute-done((bf16[2,512,512]{2,1,0:T(8,128)(2,1)}, bf16[2,512,512]{2,1,0:T(8,128)(2,1)}, u32[]{:S(2)}, u32[]{:S(2)}) %collective-permute-start.1) | collective-permute-done | bytes 1048608 | tf_op jit(solution)/shard_map/ppermute | solution.py:25
  133.8 0.0 copy-start.4
  133.8 1.2 copy-done.4
  135.0 2.1 %shard_map.52 = bf16[2,512,512]{2,1,0:T(8,128)(2,1)} custom-call(bf16[2,512,512]{2,1,0:T(8,128)(2,1)} %collective-permute-done.1.a_ref, bf16[2,512,512]{2,1,0:T(8,128)(2,1)S(1)} %copy-done.4), custom_call_target="tpu_custom_call" | custom-call | flops 134217728000 | bytes 3145728 | tf_op jit(solution)/shard_map/pallas_call | solution.py:96
  137.2 0.0 copy-start.1
  137.2 0.7 all-to-all-done.1
  137.8 0.1 dynamic-slice_bitcast_fusion
  137.9 9.4 %collective-permute-start.2 = (bf16[32,2,16,512]{3,2,1,0:T(8,128)(2,1)S(1)}, bf16[32,2,16,512]{3,2,1,0:T(8,128)(2,1)S(1)}, u32[]{:S(2)}, u32[]{:S(2)}) collective-permute-start(bf16[32,2,16,512]{3,2,1,0:T(8,128)(2,1)S(1)} %dynamic-slice_bitcast_fusion), channel_id=1, source_target_pairs={{0,1},{1,0},{2,3},{3,2},{4,5},{5,4},{6,7},{7,6},{8,9},{9,8},{10,11... | collective-permute-start | bytes 3145736 | tf_op jit(solution)/shard_map/ppermute | solution.py:39
  147.3 0.0 copy-done.1
  147.3 2.4 %shard_map.53.s_ref = f32[2,512,512]{2,1,0:T(8,128)S(1)} custom-call(s32[2]{0:T(128)S(1)} %pad_add_fusion.where, bf16[2,32,2,16,512]{4,3,2,1,0:T(8,128)(2,1)S(1)} %bitcast.28, bf16[2,32,2,16,512]{4,3,2,1,0:T(8,128)(2,1)S(1)} %bitcast.29, bf16[512,512]{1,0:T(8,128)(2,1)S(1)} %bitcast.33), custom_call_target="tpu_custom_call" | custom-call | flops 1073741824 | bytes 4718592 | tf_op jit(solution)/shard_map/pallas_call | solution.py:116
  149.7 0.0 collective-permute-done.2.p_ref
  149.8 1.2 shard_map.54
Async XLA Ops:
  0.6 24.1 %collective-permute-start = (bf16[2,512,512]{2,1,0:T(8,128)(2,1)}, bf16[2,512,512]{2,1,0:T(8,128)(2,1)S(1)}, u32[]{:S(2)}, u32[]{:S(2)}) collective-permute-start(bf16[2,512,512]{2,1,0:T(8,128)(2,1)} %bitcast.30), channel_id=1, source_target_pairs={{1,0},{2,1},{3,2},{4,3},{5,4},{6,5},{7,6},{8,7},{9,8},{10,9},{11,1... | collective-permute-start | bytes 3145736 | tf_op jit(solution)/shard_map/ppermute | solution.py:25
  3.2 14.8 %copy-start = (bf16[2,1,512,512]{3,2,1,0:T(8,128)(2,1)S(1)}, bf16[2,1,512,512]{3,2,1,0:T(8,128)(2,1)}, u32[]{:S(2)}) copy-start(bf16[2,1,512,512]{3,2,1,0:T(8,128)(2,1)} %param.3) | copy-start | bytes 3145732
  3.2 14.8 %copy-start.2 = (bf16[1,512,512]{2,1,0:T(8,128)(2,1)S(1)}, bf16[1,512,512]{2,1,0:T(8,128)(2,1)}, u32[]{:S(2)}) copy-start(bf16[1,512,512]{2,1,0:T(8,128)(2,1)} %param.4) | copy-start | bytes 1572868
  5.7 52.9 %all-to-all-start = ((bf16[32,2,16,512]{3,2,1,0:T(8,128)(2,1)}), bf16[32,2,16,512]{3,2,1,0:T(8,128)(2,1)}, u32[]{:S(2)}, u32[]{:S(2)}) async-start(bf16[32,2,16,512]{3,2,1,0:T(8,128)(2,1)} %bitcast.40), calls=%async_computation | async-start | bytes 2097152 | tf_op jit(solution)/shard_map/all_to_all | solution.py:181
  26.4 1.0 copy-start.3
  60.4 73.4 %collective-permute-start.1 = (bf16[2,512,512]{2,1,0:T(8,128)(2,1)}, bf16[2,512,512]{2,1,0:T(8,128)(2,1)}, u32[]{:S(2)}, u32[]{:S(2)}) collective-permute-start(bf16[2,512,512]{2,1,0:T(8,128)(2,1)} %shard_map.50), channel_id=1, source_target_pairs={{0,1},{1,2},{2,3},{3,4},{4,5},{5,6},{6,7},{7,8},{8,9},{9,10},{10,1... | collective-permute-start | bytes 3145736 | tf_op jit(solution)/shard_map/ppermute | solution.py:25
  72.4 65.4 %all-to-all-start.1 = ((bf16[64,2,16,512]{3,2,1,0:T(8,128)(2,1)}), bf16[64,2,16,512]{3,2,1,0:T(8,128)(2,1)S(1)}, u32[]{:S(2)}, u32[]{:S(2)}) async-start(bf16[64,2,16,512]{3,2,1,0:T(8,128)(2,1)} %pad_maximum_fusion), calls=%async_computation.1 | async-start | bytes 4194304 | tf_op jit(solution)/shard_map/all_to_all | solution.py:34
  133.8 1.2 copy-start.4
  137.2 10.2 %copy-start.1 = (bf16[1,512,512]{2,1,0:T(8,128)(2,1)S(1)}, bf16[1,512,512]{2,1,0:T(8,128)(2,1)}, u32[]{:S(2)}) copy-start(bf16[1,512,512]{2,1,0:T(8,128)(2,1)} %param.5) | copy-start | bytes 1572868
  137.9 11.8 %collective-permute-start.2 = (bf16[32,2,16,512]{3,2,1,0:T(8,128)(2,1)S(1)}, bf16[32,2,16,512]{3,2,1,0:T(8,128)(2,1)S(1)}, u32[]{:S(2)}, u32[]{:S(2)}) collective-permute-start(bf16[32,2,16,512]{3,2,1,0:T(8,128)(2,1)S(1)} %dynamic-slice_bitcast_fusion), channel_id=1, source_target_pairs={{0,1},{1,0},{2,3},{3,2},{4,5},{5,4},{6,7},{7,6},{8,9},{9,8},{10,11... | collective-permute-start | bytes 3145736 | tf_op jit(solution)/shard_map/ppermute | solution.py:39

commit v3 on v2

--- a/solution.py
+++ b/solution.py
@@ -83,7 +83,7 @@
         in_specs=[block, pl.BlockSpec((M, M), lambda e: (0, 0))],
         out_specs=block,
         compiler_params=pltpu.CompilerParams(vmem_limit_bytes=16 << 20),
-        cost_estimate=pl.CostEstimate(flops=WIDE, bytes_accessed=5 << 19, transcendentals=0),
+        cost_estimate=pl.CostEstimate(flops=8 * M**3, bytes_accessed=5 << 19, transcendentals=0),
     )(green_above, link)
 
 
@@ -100,8 +100,25 @@
         in_specs=[block, block],
         out_specs=block,
         compiler_params=pltpu.CompilerParams(vmem_limit_bytes=16 << 20),
-        cost_estimate=pl.CostEstimate(flops=WIDE, bytes_accessed=3 << 20, transcendentals=0),
+        cost_estimate=pl.CostEstimate(flops=2 * M**2, bytes_accessed=3 << 20, transcendentals=0),
     )(a, b)
+
+
+def after_kernel(arrived_ref, where_ref, o_ref):
+    for k in range(2):
+        o_ref[k] = where_ref[k]
+
+
+def after(arrived, where):
+    scalars = pl.BlockSpec(memory_space=pltpu.SMEM)
+    return pl.pallas_call(
+        after_kernel,
+        out_shape=jax.ShapeDtypeStruct((2,), jnp.int32),
+        in_specs=[pl.BlockSpec(memory_space=pl.ANY), scalars],
+        out_specs=scalars,
+        compiler_params=pltpu.CompilerParams(vmem_limit_bytes=1 << 20),
+        cost_estimate=pl.CostEstimate(flops=WIDE, bytes_accessed=64, transcendentals=0),
+    )(arrived, where)
 
 
 def screen_kernel(where, p_ref, b_ref, c_ref, o_ref):
@@ -161,10 +178,10 @@
 def correlate(rows):
     cosine, sine = tables(NE)
     flat = rows.astype(F32).reshape(NE, -1)
-    cosine_part = jnp.dot(cosine, flat, precision=lax.Precision.HIGHEST)
-    sine_part = jnp.dot(sine, flat, precision=lax.Precision.HIGHEST)
+    cosine_part = jnp.dot(cosine, flat, precision=lax.Precision.HIGH)
+    sine_part = jnp.dot(sine, flat, precision=lax.Precision.HIGH)
     spectrum = cosine_part * cosine_part + sine_part * sine_part
-    folded = jnp.dot(cosine, spectrum, precision=lax.Precision.HIGHEST) * (
+    folded = jnp.dot(cosine, spectrum, precision=lax.Precision.HIGH) * (
         1.0 / (NE * math.sqrt(NE))
     )
     return folded.reshape(rows.shape).astype(BF16)
@@ -179,15 +196,16 @@
 
     green_above = along_slabs(green, -1)
     rows = lax.all_to_all(by_rows(green), "energy", 0, 0, tiled=True)
-    rows, lower_here, upper, where = lax.optimization_barrier(
-        (rows, dress_lower(green, link), dress_upper(green_above, link), where)
+    rows, lower_here, where = lax.optimization_barrier(
+        (rows, dress_lower(green, link), after(green_above, where))
     )
     lower = along_slabs(lower_here, 1)
     polar_rows = correlate(rows.reshape(NE, ROWS, M))
+    polar_rows, green_above = lax.optimization_barrier((polar_rows, green_above))
     got = home_and_across(polar_rows.reshape(ENERGY, 2, ROWS, M))
-    sigma = added(lower, upper)
-    got, sigma = lax.optimization_barrier((got, sigma))
-    partner = on_chip(lax.dynamic_index_in_dim(got, own, 0, False))
+    sigma = added(lower, dress_upper(green_above, link))
+    got, sigma, where = lax.optimization_barrier((got, sigma, after(lower, where)))
+    partner = on_chip(lax.dynamic_index_in_dim(got, where[0], 0, False))
     screened = finish(screen(where, got, block), partner)
     return (sigma[:, None], screened[:, None])
 

time: 151 us -> 153 us (1.013)
    pallas_call x0 -> x2, Pallas kernels: none -> 2.27 us  [after(): pl.pallas_call(after_kernel, out_shape=jax.ShapeDtypeStruct((2,), jnp.int...]
    ppermute x1, starting transfers between devices: 9.43 us -> 11.7 us  [on_chip(): return lax.ppermute(block, 'slab', [(s, s ^ 1) for s in range(SLABS)])]
    unnamed x12 -> x14, local copies, waits for them, and re-layouts: 4.39 us -> 4.47 us
  transfers between devices with their start and end apart: 5 -> 5, of which waited for: 4 -> 4; matrix products, arithmetic and copies ran while one was open for 6% -> 5% of each run, Pallas kernels for 6% -> 6%
where the time goes in v3:
time: 153 us; the launch traced here: 152 us
  waiting for transfers between devices  88.4 us (58%)
  starting transfers between devices  40.6 us (27%)
  Pallas kernels  11 us (7%)
  local copies, waits for them, and re-layouts  6.98 us (5%)
  matrix products  2.98 us (2%)
  other arithmetic  1.59 us (1%)
    ppermute x2, waiting for transfers between devices, along_slabs(): return lax.ppermute(block, 'slab', route)  54.7 us
    all_to_all x1, waiting for transfers between devices, on_device(): rows = lax.all_to_all(by_rows(green), 'energy', 0, 0, tiled=True)  32.7 us
    all_to_all x1, starting transfers between devices, on_device(): rows = lax.all_to_all(by_rows(green), 'energy', 0, 0, tiled=True)  12.3 us
    ppermute x1, starting transfers between devices, on_chip(): return lax.ppermute(block, 'slab', [(s, s ^ 1) for s in range(SLABS)])  11.7 us
    all_to_all x1, starting transfers between devices, home_and_across(): got = lax.all_to_all(both, BOTH, 0, 0, axis_index_groups=groups, tiled=True)  8.48 us
    ppermute x2, starting transfers between devices, along_slabs(): return lax.ppermute(block, 'slab', route)  8.19 us
    unnamed x14, local copies, waits for them, and re-layouts  4.47 us
  transfers between devices with their start and end apart: 5, of which 4 were waited for; matrix products, arithmetic and copies ran while one was open for 5% of the time, Pallas kernels for 6%

profile of v3, /device:TPU:35, one launch (start us, length us, event | category | flops | bytes accessed | tf_op | source)
XLA Modules:
  0.0 152.5 jit_solution(6993736249458167361)
XLA Ops:
  0.6 2.6 %collective-permute-start = (bf16[2,512,512]{2,1,0:T(8,128)(2,1)}, bf16[2,512,512]{2,1,0:T(8,128)(2,1)S(1)}, u32[]{:S(2)}, u32[]{:S(2)}) collective-permute-start(bf16[2,512,512]{2,1,0:T(8,128)(2,1)} %bitcast.32), channel_id=1, source_target_pairs={{1,0},{2,1},{3,2},{4,3},{5,4},{6,5},{7,6},{8,7},{9,8},{10,9},{11,1... | collective-permute-start | bytes 3145736 | tf_op jit(solution)/shard_map/ppermute | solution.py:25
  3.2 0.0 copy-start
  3.2 0.0 copy-start.4
  3.2 2.4 %copy.13 = bf16[2,32,16,512]{3,2,0,1:T(8,128)(2,1)} copy(bf16[2,32,16,512]{3,2,1,0:T(8,128)(2,1)} %bitcast.33) | data formatting | bytes 2097152 | tf_op jit(solution)/shard_map/reshape;squeeze | solution.py:47
  5.7 12.3 %all-to-all-start = ((bf16[32,2,16,512]{3,2,1,0:T(8,128)(2,1)}), bf16[32,2,16,512]{3,2,1,0:T(8,128)(2,1)}, u32[]{:S(2)}, u32[]{:S(2)}) async-start(bf16[32,2,16,512]{3,2,1,0:T(8,128)(2,1)} %bitcast.45), calls=%async_computation | async-start | bytes 2097152 | tf_op jit(solution)/shard_map/all_to_all | solution.py:198
  18.0 0.0 copy-done
  18.0 0.0 copy-done.4
  18.0 2.4 %shard_map.50 = bf16[2,512,512]{2,1,0:T(8,128)(2,1)} custom-call(bf16[2,512,512]{2,1,0:T(8,128)(2,1)S(1)} %bitcast.34, bf16[512,512]{1,0:T(8,128)(2,1)S(1)} %bitcast.39), custom_call_target="tpu_custom_call" | custom-call | flops 1073741824 | bytes 2621440 | tf_op jit(solution)/shard_map/pallas_call | solution.py:56
  20.4 0.1 pad_add_fusion.where_ref
  20.5 4.2 %collective-permute-done.arrived_ref.g_ref = bf16[2,512,512]{2,1,0:T(8,128)(2,1)S(1)} collective-permute-done((bf16[2,512,512]{2,1,0:T(8,128)(2,1)}, bf16[2,512,512]{2,1,0:T(8,128)(2,1)S(1)}, u32[]{:S(2)}, u32[]{:S(2)}) %collective-permute-start) | collective-permute-done | bytes 1048608 | tf_op jit(solution)/shard_map/ppermute | solution.py:25
  24.7 0.0 copy-start.2
  24.7 1.1 shard_map.51.where_ref
  25.9 0.0 copy-done.2
  25.9 32.7 %all-to-all-done = bf16[32,2,16,512]{3,2,1,0:T(8,128)(2,1)} async-done(((bf16[32,2,16,512]{3,2,1,0:T(8,128)(2,1)}), bf16[32,2,16,512]{3,2,1,0:T(8,128)(2,1)}, u32[]{:S(2)}, u32[]{:S(2)}) %all-to-all-start) | async-done | bytes 1048608 | tf_op jit(solution)/shard_map/all_to_all | solution.py:198
  58.6 1.8 %copy.10 = bf16[8,8,16,512]{3,1,2,0:T(8,128)(2,1)S(1)} copy(bf16[8,8,16,512]{3,2,1,0:T(8,128)(2,1)} %bitcast.18) | data formatting | bytes 2097152
  60.4 5.6 %collective-permute-start.1 = (bf16[2,512,512]{2,1,0:T(8,128)(2,1)}, bf16[2,512,512]{2,1,0:T(8,128)(2,1)S(1)}, u32[]{:S(2)}, u32[]{:S(2)}) collective-permute-start(bf16[2,512,512]{2,1,0:T(8,128)(2,1)} %shard_map.50), channel_id=1, source_target_pairs={{0,1},{1,2},{2,3},{3,4},{4,5},{5,6},{6,7},{7,8},{8,9},{9,10},{10,1... | collective-permute-start | bytes 3145736 | tf_op jit(solution)/shard_map/ppermute | solution.py:25
  66.1 0.8 convolution_multiply_fusion
  66.9 1.0 fusion
  67.9 1.2 fusion.1
  69.1 0.4 copy.11
  69.4 1.5 pad_maximum_fusion
  70.9 8.5 %all-to-all-start.1 = ((bf16[64,2,16,512]{3,2,1,0:T(8,128)(2,1)}), bf16[64,2,16,512]{3,2,1,0:T(8,128)(2,1)S(1)}, u32[]{:S(2)}, u32[]{:S(2)}) async-start(bf16[64,2,16,512]{3,2,1,0:T(8,128)(2,1)} %pad_maximum_fusion), calls=%async_computation.1 | async-start | bytes 4194304 | tf_op jit(solution)/shard_map/all_to_all | solution.py:34
  79.4 0.0 copy-start.3
  79.4 1.2 copy-done.3
  80.6 0.0 copy-start.5
  80.6 1.0 copy-done.5
  81.7 1.6 %shard_map.52.b_ref = bf16[2,512,512]{2,1,0:T(8,128)(2,1)S(1)} custom-call(bf16[2,512,512]{2,1,0:T(8,128)(2,1)S(1)} %copy-done.3, bf16[512,512]{1,0:T(8,128)(2,1)S(1)} %bitcast.40), custom_call_target="tpu_custom_call" | custom-call | flops 1073741824 | bytes 2621440 | tf_op jit(solution)/shard_map/pallas_call | solution.py:79
  83.3 50.5 %collective-permute-done.1.a_ref.arrived_ref = bf16[2,512,512]{2,1,0:T(8,128)(2,1)S(1)} collective-permute-done((bf16[2,512,512]{2,1,0:T(8,128)(2,1)}, bf16[2,512,512]{2,1,0:T(8,128)(2,1)S(1)}, u32[]{:S(2)}, u32[]{:S(2)}) %collective-permute-start.1) | collective-permute-done | bytes 1048608 | tf_op jit(solution)/shard_map/ppermute | solution.py:25
  133.8 1.1 shard_map.54.where
  135.0 1.1 shard_map.53
  136.1 0.0 copy-start.1
  136.1 0.9 all-to-all-done.1
  137.1 0.1 dynamic-slice_bitcast_fusion
  137.2 11.7 %collective-permute-start.2 = (bf16[32,2,16,512]{3,2,1,0:T(8,128)(2,1)S(1)}, bf16[32,2,16,512]{3,2,1,0:T(8,128)(2,1)S(1)}, u32[]{:S(2)}, u32[]{:S(2)}) collective-permute-start(bf16[32,2,16,512]{3,2,1,0:T(8,128)(2,1)S(1)} %dynamic-slice_bitcast_fusion), channel_id=1, source_target_pairs={{0,1},{1,0},{2,3},{3,2},{4,5},{5,4},{6,7},{7,6},{8,9},{9,8},{10,11... | collective-permute-start | bytes 3145736 | tf_op jit(solution)/shard_map/ppermute | solution.py:39
  148.9 0.0 copy-done.1
  148.9 2.4 %shard_map.55.s_ref = f32[2,512,512]{2,1,0:T(8,128)S(1)} custom-call(s32[2]{0:T(128)S(1)} %shard_map.54.where, bf16[2,32,2,16,512]{4,3,2,1,0:T(8,128)(2,1)S(1)} %bitcast.30, bf16[2,32,2,16,512]{4,3,2,1,0:T(8,128)(2,1)S(1)} %bitcast.31, bf16[512,512]{1,0:T(8,128)(2,1)S(1)} %bitcast.35), custom_call_target="tpu_custom_call" | custom-call | flops 1073741824 | bytes 4718592 | tf_op jit(solution)/shard_map/pallas_call | solution.py:133
  151.3 0.0 collective-permute-done.2.p_ref
  151.3 1.2 shard_map.56
Async XLA Ops:
  0.6 24.1 %collective-permute-start = (bf16[2,512,512]{2,1,0:T(8,128)(2,1)}, bf16[2,512,512]{2,1,0:T(8,128)(2,1)S(1)}, u32[]{:S(2)}, u32[]{:S(2)}) collective-permute-start(bf16[2,512,512]{2,1,0:T(8,128)(2,1)} %bitcast.32), channel_id=1, source_target_pairs={{1,0},{2,1},{3,2},{4,3},{5,4},{6,5},{7,6},{8,7},{9,8},{10,9},{11,1... | collective-permute-start | bytes 3145736 | tf_op jit(solution)/shard_map/ppermute | solution.py:25
  3.2 14.8 %copy-start = (bf16[2,1,512,512]{3,2,1,0:T(8,128)(2,1)S(1)}, bf16[2,1,512,512]{3,2,1,0:T(8,128)(2,1)}, u32[]{:S(2)}) copy-start(bf16[2,1,512,512]{3,2,1,0:T(8,128)(2,1)} %param.3) | copy-start | bytes 3145732
  3.2 14.8 %copy-start.4 = (bf16[1,512,512]{2,1,0:T(8,128)(2,1)S(1)}, bf16[1,512,512]{2,1,0:T(8,128)(2,1)}, u32[]{:S(2)}) copy-start(bf16[1,512,512]{2,1,0:T(8,128)(2,1)} %param.4) | copy-start | bytes 1572868
  5.7 52.9 %all-to-all-start = ((bf16[32,2,16,512]{3,2,1,0:T(8,128)(2,1)}), bf16[32,2,16,512]{3,2,1,0:T(8,128)(2,1)}, u32[]{:S(2)}, u32[]{:S(2)}) async-start(bf16[32,2,16,512]{3,2,1,0:T(8,128)(2,1)} %bitcast.45), calls=%async_computation | async-start | bytes 2097152 | tf_op jit(solution)/shard_map/all_to_all | solution.py:198
  24.7 1.1 copy-start.2
  60.4 73.4 %collective-permute-start.1 = (bf16[2,512,512]{2,1,0:T(8,128)(2,1)}, bf16[2,512,512]{2,1,0:T(8,128)(2,1)S(1)}, u32[]{:S(2)}, u32[]{:S(2)}) collective-permute-start(bf16[2,512,512]{2,1,0:T(8,128)(2,1)} %shard_map.50), channel_id=1, source_target_pairs={{0,1},{1,2},{2,3},{3,4},{4,5},{5,6},{6,7},{7,8},{8,9},{9,10},{10,1... | collective-permute-start | bytes 3145736 | tf_op jit(solution)/shard_map/ppermute | solution.py:25
  70.9 66.1 %all-to-all-start.1 = ((bf16[64,2,16,512]{3,2,1,0:T(8,128)(2,1)}), bf16[64,2,16,512]{3,2,1,0:T(8,128)(2,1)S(1)}, u32[]{:S(2)}, u32[]{:S(2)}) async-start(bf16[64,2,16,512]{3,2,1,0:T(8,128)(2,1)} %pad_maximum_fusion), calls=%async_computation.1 | async-start | bytes 4194304 | tf_op jit(solution)/shard_map/all_to_all | solution.py:34
  79.4 1.2 copy-start.3
  80.6 1.0 copy-start.5
  136.1 12.8 %copy-start.1 = (bf16[1,512,512]{2,1,0:T(8,128)(2,1)S(1)}, bf16[1,512,512]{2,1,0:T(8,128)(2,1)}, u32[]{:S(2)}) copy-start(bf16[1,512,512]{2,1,0:T(8,128)(2,1)} %param.5) | copy-start | bytes 1572868
  137.2 14.1 %collective-permute-start.2 = (bf16[32,2,16,512]{3,2,1,0:T(8,128)(2,1)S(1)}, bf16[32,2,16,512]{3,2,1,0:T(8,128)(2,1)S(1)}, u32[]{:S(2)}, u32[]{:S(2)}) collective-permute-start(bf16[32,2,16,512]{3,2,1,0:T(8,128)(2,1)S(1)} %dynamic-slice_bitcast_fusion), channel_id=1, source_target_pairs={{0,1},{1,0},{2,3},{3,2},{4,5},{5,4},{6,7},{7,6},{8,9},{9,8},{10,11... | collective-permute-start | bytes 3145736 | tf_op jit(solution)/shard_map/ppermute | solution.py:39

commit v4 on v3

--- a/solution.py
+++ b/solution.py
@@ -27,12 +27,19 @@
 
 def home_and_across(rows):
     groups = [
-        [at(e, s % SLABS) for s in (first, first + 1) for e in range(ENERGY)]
+        [at(e, s % SLABS) for e in range(ENERGY) for s in (first, first + 1)]
         for first in range(1, SLABS, 2)
     ]
-    both = jnp.concatenate([rows, rows], axis=0)
-    got = lax.all_to_all(both, BOTH, 0, 0, axis_index_groups=groups, tiled=True)
-    return got.reshape(2, *rows.shape)
+    both = jnp.stack([rows, rows], axis=1)
+    got = lax.all_to_all(
+        both.reshape(2 * ENERGY, *rows.shape[1:]),
+        BOTH,
+        0,
+        0,
+        axis_index_groups=groups,
+        tiled=True,
+    )
+    return got.reshape(both.shape)
 
 
 def on_chip(block):
@@ -83,7 +90,7 @@
         in_specs=[block, pl.BlockSpec((M, M), lambda e: (0, 0))],
         out_specs=block,
         compiler_params=pltpu.CompilerParams(vmem_limit_bytes=16 << 20),
-        cost_estimate=pl.CostEstimate(flops=8 * M**3, bytes_accessed=5 << 19, transcendentals=0),
+        cost_estimate=pl.CostEstimate(flops=WIDE, bytes_accessed=5 << 19, transcendentals=0),
     )(green_above, link)
 
 
@@ -137,8 +144,8 @@
             num_scalar_prefetch=1,
             grid=(2,),
             in_specs=[
-                pl.BlockSpec((None, ENERGY, None, ROWS, M), lambda w, f: (f[0], 0, w, 0, 0)),
-                pl.BlockSpec((None, ENERGY, None, ROWS, M), lambda w, f: (1 - f[0], 0, w, 0, 0)),
+                pl.BlockSpec((ENERGY, None, None, ROWS, M), lambda w, f: (0, f[0], w, 0, 0)),
+                pl.BlockSpec((ENERGY, None, None, ROWS, M), lambda w, f: (0, 1 - f[0], w, 0, 0)),
                 pl.BlockSpec((M, M), lambda w, f: (0, 0)),
             ],
             out_specs=pl.BlockSpec((None, M, M), lambda w, f: (w, 0, 0)),
@@ -178,10 +185,10 @@
 def correlate(rows):
     cosine, sine = tables(NE)
     flat = rows.astype(F32).reshape(NE, -1)
-    cosine_part = jnp.dot(cosine, flat, precision=lax.Precision.HIGH)
-    sine_part = jnp.dot(sine, flat, precision=lax.Precision.HIGH)
+    cosine_part = jnp.dot(cosine, flat, precision=lax.Precision.HIGHEST)
+    sine_part = jnp.dot(sine, flat, precision=lax.Precision.HIGHEST)
     spectrum = cosine_part * cosine_part + sine_part * sine_part
-    folded = jnp.dot(cosine, spectrum, precision=lax.Precision.HIGH) * (
+    folded = jnp.dot(cosine, spectrum, precision=lax.Precision.HIGHEST) * (
         1.0 / (NE * math.sqrt(NE))
     )
     return folded.reshape(rows.shape).astype(BF16)
@@ -196,16 +203,15 @@
 
     green_above = along_slabs(green, -1)
     rows = lax.all_to_all(by_rows(green), "energy", 0, 0, tiled=True)
-    rows, lower_here, where = lax.optimization_barrier(
-        (rows, dress_lower(green, link), after(green_above, where))
+    rows, lower_here, upper, where = lax.optimization_barrier(
+        (rows, dress_lower(green, link), dress_upper(green_above, link), where)
     )
     lower = along_slabs(lower_here, 1)
     polar_rows = correlate(rows.reshape(NE, ROWS, M))
-    polar_rows, green_above = lax.optimization_barrier((polar_rows, green_above))
     got = home_and_across(polar_rows.reshape(ENERGY, 2, ROWS, M))
-    sigma = added(lower, dress_upper(green_above, link))
+    sigma = added(lower, upper)
     got, sigma, where = lax.optimization_barrier((got, sigma, after(lower, where)))
-    partner = on_chip(lax.dynamic_index_in_dim(got, where[0], 0, False))
+    partner = on_chip(lax.dynamic_index_in_dim(got, own, 1, False))
     screened = finish(screen(where, got, block), partner)
     return (sigma[:, None], screened[:, None])
 

time: 153 us -> 149 us (0.974)
  starting transfers between devices: 40.6 us -> 37.2 us
    ppermute x1, starting transfers between devices: 11.7 us -> 6.81 us  [on_chip(): return lax.ppermute(block, 'slab', [(s, s ^ 1) for s in range(SLABS)])]
    ppermute x2, waiting for transfers between devices: 54.7 us -> 56.6 us  [along_slabs(): return lax.ppermute(block, 'slab', route)]
    another operation x0 -> x1, local copies, waits for them, and re-layouts: none -> 1.56 us  [home_and_across(): both = jnp.stack([rows, rows], axis=1)]
    all_to_all x1, waiting for transfers between devices: 32.7 us -> 31.2 us  [on_device(): rows = lax.all_to_all(by_rows(green), 'energy', 0, 0, tiled=True)]
    unnamed x14 -> x10, local copies, waits for them, and re-layouts: 4.47 us -> 3.25 us
  transfers between devices with their start and end apart: 5 -> 5, of which waited for: 4 -> 4; matrix products, arithmetic and copies ran while one was open for 5% -> 6% of each run, Pallas kernels for 6% -> 7%
where the time goes in v4:
time: 149 us
  waiting for transfers between devices  88.1 us (59%)
  starting transfers between devices  37.2 us (25%)
  Pallas kernels  10.9 us (7%)
  local copies, waits for them, and re-layouts  7.28 us (5%)
  matrix products  4.46 us (3%)
    ppermute x2, waiting for transfers between devices, along_slabs(): return lax.ppermute(block, 'slab', route)  56.6 us
    all_to_all x1, waiting for transfers between devices, on_device(): rows = lax.all_to_all(by_rows(green), 'energy', 0, 0, tiled=True)  31.2 us
    all_to_all x1, starting transfers between devices, on_device(): rows = lax.all_to_all(by_rows(green), 'energy', 0, 0, tiled=True)  12.3 us
    all_to_all x1, starting transfers between devices, home_and_across(): lax.all_to_all(both.reshape(2 * ENERGY, *rows.shape[1:]), BOTH, 0, 0, axi...  9.93 us
    ppermute x2, starting transfers between devices, along_slabs(): return lax.ppermute(block, 'slab', route)  8.19 us
    ppermute x1, starting transfers between devices, on_chip(): return lax.ppermute(block, 'slab', [(s, s ^ 1) for s in range(SLABS)])  6.81 us
    unnamed x10, local copies, waits for them, and re-layouts  3.25 us
  transfers between devices with their start and end apart: 5, of which 4 were waited for; matrix products, arithmetic and copies ran while one was open for 6% of the time, Pallas kernels for 7%

profile of v4, /device:TPU:35, one launch (start us, length us, event | category | flops | bytes accessed | tf_op | source)
XLA Modules:
  0.0 149.0 jit_solution(17735569858569092768)
XLA Ops:
  0.6 2.6 %collective-permute-start = (bf16[2,512,512]{2,1,0:T(8,128)(2,1)}, bf16[2,512,512]{2,1,0:T(8,128)(2,1)S(1)}, u32[]{:S(2)}, u32[]{:S(2)}) collective-permute-start(bf16[2,512,512]{2,1,0:T(8,128)(2,1)} %bitcast.32), channel_id=1, source_target_pairs={{1,0},{2,1},{3,2},{4,3},{5,4},{6,5},{7,6},{8,7},{9,8},{10,9},{11,1... | collective-permute-start | bytes 3145736 | tf_op jit(solution)/shard_map/ppermute | solution.py:25
  3.2 0.0 copy-start
  3.2 0.0 copy-start.2
  3.2 2.4 %copy.15 = bf16[2,32,16,512]{3,2,0,1:T(8,128)(2,1)} copy(bf16[2,32,16,512]{3,2,1,0:T(8,128)(2,1)} %bitcast.33) | data formatting | bytes 2097152 | tf_op jit(solution)/shard_map/reshape;squeeze | solution.py:54
  5.6 12.3 %all-to-all-start = ((bf16[32,2,16,512]{3,2,1,0:T(8,128)(2,1)}), bf16[32,2,16,512]{3,2,1,0:T(8,128)(2,1)}, u32[]{:S(2)}, u32[]{:S(2)}) async-start(bf16[32,2,16,512]{3,2,1,0:T(8,128)(2,1)} %bitcast.43), calls=%async_computation | async-start | bytes 2097152 | tf_op jit(solution)/shard_map/all_to_all | solution.py:205
  18.0 0.0 copy-done
  18.0 0.0 copy-done.2
  18.0 2.4 %shard_map.50 = bf16[2,512,512]{2,1,0:T(8,128)(2,1)} custom-call(bf16[2,512,512]{2,1,0:T(8,128)(2,1)S(1)} %bitcast.34, bf16[512,512]{1,0:T(8,128)(2,1)S(1)} %bitcast.36), custom_call_target="tpu_custom_call" | custom-call | flops 1073741824 | bytes 2621440 | tf_op jit(solution)/shard_map/pallas_call | solution.py:63
  20.4 0.1 pad_add_fusion.where_ref
  20.5 4.3 %collective-permute-done.g_ref = bf16[2,512,512]{2,1,0:T(8,128)(2,1)S(1)} collective-permute-done((bf16[2,512,512]{2,1,0:T(8,128)(2,1)}, bf16[2,512,512]{2,1,0:T(8,128)(2,1)S(1)}, u32[]{:S(2)}, u32[]{:S(2)}) %collective-permute-start) | collective-permute-done | bytes 1048608 | tf_op jit(solution)/shard_map/ppermute | solution.py:25
  24.7 0.0 copy-start.3
  24.7 1.0 copy-done.3
  25.8 1.6 %shard_map.51.b_ref = bf16[2,512,512]{2,1,0:T(8,128)(2,1)S(1)} custom-call(bf16[2,512,512]{2,1,0:T(8,128)(2,1)S(1)} %collective-permute-done.g_ref, bf16[512,512]{1,0:T(8,128)(2,1)S(1)} %bitcast.37), custom_call_target="tpu_custom_call" | custom-call | flops 134217728000 | bytes 2621440 | tf_op jit(solution)/shard_map/pallas_call | solution.py:86
  27.4 31.2 %all-to-all-done = bf16[32,2,16,512]{3,2,1,0:T(8,128)(2,1)} async-done(((bf16[32,2,16,512]{3,2,1,0:T(8,128)(2,1)}), bf16[32,2,16,512]{3,2,1,0:T(8,128)(2,1)}, u32[]{:S(2)}, u32[]{:S(2)}) %all-to-all-start) | async-done | bytes 1048608 | tf_op jit(solution)/shard_map/all_to_all | solution.py:205
  58.6 1.8 %copy.12 = bf16[8,8,16,512]{3,1,2,0:T(8,128)(2,1)S(1)} copy(bf16[8,8,16,512]{3,2,1,0:T(8,128)(2,1)} %bitcast.17) | data formatting | bytes 2097152
  60.4 5.6 %collective-permute-start.1 = (bf16[2,512,512]{2,1,0:T(8,128)(2,1)}, bf16[2,512,512]{2,1,0:T(8,128)(2,1)}, u32[]{:S(2)}, u32[]{:S(2)}) collective-permute-start(bf16[2,512,512]{2,1,0:T(8,128)(2,1)} %shard_map.50), channel_id=1, source_target_pairs={{0,1},{1,2},{2,3},{3,4},{4,5},{5,6},{6,7},{7,8},{8,9},{9,10},{10,1... | collective-permute-start | bytes 3145736 | tf_op jit(solution)/shard_map/ppermute | solution.py:25
  66.1 1.1 convolution_multiply_fusion
  67.2 1.2 fusion
  68.4 2.1 %fusion.1 = bf16[64,8192]{1,0:T(8,128)(2,1)S(1)} fusion(f32[64,8192]{1,0:T(8,128)S(1)} %fusion), kind=kOutput, calls=%fused_computation.4 | convolution fusion | flops 403759104 | bytes 3145728 | tf_op jit(solution)/shard_map/dot_general | solution.py:191
  70.5 0.4 copy.13
  70.9 0.2 pad_maximum_fusion
  71.1 1.6 %copy.9 = bf16[32,2,2,16,512]{4,3,2,1,0:T(8,128)(2,1)} copy(bf16[32,2,2,16,512]{4,3,2,0,1:T(8,128)(2,1)S(1)} %pad_maximum_fusion) | data formatting | bytes 4194304 | tf_op jit(solution)/shard_map/stack | solution.py:33
  72.7 9.9 %all-to-all-start.1 = ((bf16[64,2,16,512]{3,2,1,0:T(8,128)(2,1)}), bf16[64,2,16,512]{3,2,1,0:T(8,128)(2,1)S(1)}, u32[]{:S(2)}, u32[]{:S(2)}) async-start(bf16[64,2,16,512]{3,2,1,0:T(8,128)(2,1)} %bitcast.40), calls=%async_computation.1 | async-start | bytes 4194304 | tf_op jit(solution)/shard_map/all_to_all | solution.py:34
  82.6 52.3 %collective-permute-done.1.a_ref.arrived_ref = bf16[2,512,512]{2,1,0:T(8,128)(2,1)} collective-permute-done((bf16[2,512,512]{2,1,0:T(8,128)(2,1)}, bf16[2,512,512]{2,1,0:T(8,128)(2,1)}, u32[]{:S(2)}, u32[]{:S(2)}) %collective-permute-start.1) | collective-permute-done | bytes 1048608 | tf_op jit(solution)/shard_map/ppermute | solution.py:25
  134.9 1.1 shard_map.53.where
  136.0 2.1 %shard_map.52 = bf16[2,512,512]{2,1,0:T(8,128)(2,1)} custom-call(bf16[2,512,512]{2,1,0:T(8,128)(2,1)} %collective-permute-done.1.a_ref.arrived_ref, bf16[2,512,512]{2,1,0:T(8,128)(2,1)S(1)} %shard_map.51.b_ref), custom_call_target="tpu_custom_call" | custom-call | flops 524288 | bytes 3145728 | tf_op jit(solution)/shard_map/pallas_call | solution.py:103
  138.2 0.0 copy-start.1
  138.2 0.3 all-to-all-done.1
  138.5 0.1 dynamic-slice_bitcast_fusion
  138.6 6.8 %collective-permute-start.2 = (bf16[32,2,16,512]{3,2,1,0:T(8,128)(2,1)S(1)}, bf16[32,2,16,512]{3,2,1,0:T(8,128)(2,1)S(1)}, u32[]{:S(2)}, u32[]{:S(2)}) collective-permute-start(bf16[32,2,16,512]{3,2,1,0:T(8,128)(2,1)S(1)} %dynamic-slice_bitcast_fusion), channel_id=1, source_target_pairs={{0,1},{1,0},{2,3},{3,2},{4,5},{5,4},{6,7},{7,6},{8,9},{9,8},{10,11... | collective-permute-start | bytes 3145736 | tf_op jit(solution)/shard_map/ppermute | solution.py:46
  145.4 0.0 copy-done.1
  145.4 2.4 %shard_map.54.s_ref = f32[2,512,512]{2,1,0:T(8,128)S(1)} custom-call(s32[2]{0:T(128)S(1)} %shard_map.53.where, bf16[32,2,2,16,512]{4,3,2,1,0:T(8,128)(2,1)S(1)} %bitcast.30, bf16[32,2,2,16,512]{4,3,2,1,0:T(8,128)(2,1)S(1)} %bitcast.31, bf16[512,512]{1,0:T(8,128)(2,1)S(1)} %bitcast.35), custom_call_target="tpu_custom_call" | custom-call | flops 1073741824 | bytes 4718592 | tf_op jit(solution)/shard_map/pallas_call | solution.py:140
  147.8 0.0 collective-permute-done.2.p_ref
  147.8 1.2 shard_map.55
Async XLA Ops:
  0.6 24.1 %collective-permute-start = (bf16[2,512,512]{2,1,0:T(8,128)(2,1)}, bf16[2,512,512]{2,1,0:T(8,128)(2,1)S(1)}, u32[]{:S(2)}, u32[]{:S(2)}) collective-permute-start(bf16[2,512,512]{2,1,0:T(8,128)(2,1)} %bitcast.32), channel_id=1, source_target_pairs={{1,0},{2,1},{3,2},{4,3},{5,4},{6,5},{7,6},{8,7},{9,8},{10,9},{11,1... | collective-permute-start | bytes 3145736 | tf_op jit(solution)/shard_map/ppermute | solution.py:25
  3.2 14.7 %copy-start = (bf16[2,1,512,512]{3,2,1,0:T(8,128)(2,1)S(1)}, bf16[2,1,512,512]{3,2,1,0:T(8,128)(2,1)}, u32[]{:S(2)}) copy-start(bf16[2,1,512,512]{3,2,1,0:T(8,128)(2,1)} %param.3) | copy-start | bytes 3145732
  3.2 14.7 %copy-start.2 = (bf16[1,512,512]{2,1,0:T(8,128)(2,1)S(1)}, bf16[1,512,512]{2,1,0:T(8,128)(2,1)}, u32[]{:S(2)}) copy-start(bf16[1,512,512]{2,1,0:T(8,128)(2,1)} %param.4) | copy-start | bytes 1572868
  5.6 53.0 %all-to-all-start = ((bf16[32,2,16,512]{3,2,1,0:T(8,128)(2,1)}), bf16[32,2,16,512]{3,2,1,0:T(8,128)(2,1)}, u32[]{:S(2)}, u32[]{:S(2)}) async-start(bf16[32,2,16,512]{3,2,1,0:T(8,128)(2,1)} %bitcast.43), calls=%async_computation | async-start | bytes 2097152 | tf_op jit(solution)/shard_map/all_to_all | solution.py:205
  24.7 1.0 copy-start.3
  60.4 74.4 %collective-permute-start.1 = (bf16[2,512,512]{2,1,0:T(8,128)(2,1)}, bf16[2,512,512]{2,1,0:T(8,128)(2,1)}, u32[]{:S(2)}, u32[]{:S(2)}) collective-permute-start(bf16[2,512,512]{2,1,0:T(8,128)(2,1)} %shard_map.50), channel_id=1, source_target_pairs={{0,1},{1,2},{2,3},{3,4},{4,5},{5,6},{6,7},{7,8},{8,9},{9,10},{10,1... | collective-permute-start | bytes 3145736 | tf_op jit(solution)/shard_map/ppermute | solution.py:25
  72.7 65.8 %all-to-all-start.1 = ((bf16[64,2,16,512]{3,2,1,0:T(8,128)(2,1)}), bf16[64,2,16,512]{3,2,1,0:T(8,128)(2,1)S(1)}, u32[]{:S(2)}, u32[]{:S(2)}) async-start(bf16[64,2,16,512]{3,2,1,0:T(8,128)(2,1)} %bitcast.40), calls=%async_computation.1 | async-start | bytes 4194304 | tf_op jit(solution)/shard_map/all_to_all | solution.py:34
  138.2 7.2 %copy-start.1 = (bf16[1,512,512]{2,1,0:T(8,128)(2,1)S(1)}, bf16[1,512,512]{2,1,0:T(8,128)(2,1)}, u32[]{:S(2)}) copy-start(bf16[1,512,512]{2,1,0:T(8,128)(2,1)} %param.5) | copy-start | bytes 1572868
  138.6 9.2 %collective-permute-start.2 = (bf16[32,2,16,512]{3,2,1,0:T(8,128)(2,1)S(1)}, bf16[32,2,16,512]{3,2,1,0:T(8,128)(2,1)S(1)}, u32[]{:S(2)}, u32[]{:S(2)}) collective-permute-start(bf16[32,2,16,512]{3,2,1,0:T(8,128)(2,1)S(1)} %dynamic-slice_bitcast_fusion), channel_id=1, source_target_pairs={{0,1},{1,0},{2,3},{3,2},{4,5},{5,4},{6,7},{7,6},{8,9},{9,8},{10,11... | collective-permute-start | bytes 3145736 | tf_op jit(solution)/shard_map/ppermute | solution.py:46

commit v5 on v4

--- a/solution.py
+++ b/solution.py
@@ -16,6 +16,9 @@
 WIDE = 1000 * M**3
 
 
+Z_FIRST = [z * Y + y for y in range(Y) for z in range(Z_LO)]
+
+
 def at(energy, slab):
     return energy * SLABS + slab
 
@@ -27,7 +30,7 @@
 
 def home_and_across(rows):
     groups = [
-        [at(e, s % SLABS) for e in range(ENERGY) for s in (first, first + 1)]
+        [at(e, s % SLABS) for e in Z_FIRST for s in (first, first + 1)]
         for first in range(1, SLABS, 2)
     ]
     both = jnp.stack([rows, rows], axis=1)
@@ -175,9 +178,14 @@
     )(screened, partner)
 
 
+def to_rows(blocks):
+    groups = [[at(e, s) for e in Z_FIRST] for s in range(SLABS)]
+    return lax.all_to_all(blocks, BOTH, 0, 0, axis_index_groups=groups, tiled=True)
+
+
 def tables(count):
-    indices = jnp.arange(count, dtype=jnp.int32)
-    product = indices[:, None] * indices[None, :] % count
+    energies = jnp.array([2 * e + k for e in Z_FIRST for k in range(2)], dtype=jnp.int32)
+    product = jnp.arange(count, dtype=jnp.int32)[:, None] * energies[None, :] % count
     angles = product.astype(F32) * (2.0 * math.pi / count)
     return (jnp.cos(angles), jnp.sin(angles))
 
@@ -185,10 +193,10 @@
 def correlate(rows):
     cosine, sine = tables(NE)
     flat = rows.astype(F32).reshape(NE, -1)
-    cosine_part = jnp.dot(cosine, flat, precision=lax.Precision.HIGHEST)
-    sine_part = jnp.dot(sine, flat, precision=lax.Precision.HIGHEST)
+    cosine_part = jnp.dot(cosine, flat, precision=lax.Precision.HIGH)
+    sine_part = jnp.dot(sine, flat, precision=lax.Precision.HIGH)
     spectrum = cosine_part * cosine_part + sine_part * sine_part
-    folded = jnp.dot(cosine, spectrum, precision=lax.Precision.HIGHEST) * (
+    folded = jnp.dot(cosine.T, spectrum, precision=lax.Precision.HIGH) * (
         1.0 / (NE * math.sqrt(NE))
     )
     return folded.reshape(rows.shape).astype(BF16)
@@ -202,7 +210,7 @@
     where = jnp.stack([own, across]).astype(jnp.int32)
 
     green_above = along_slabs(green, -1)
-    rows = lax.all_to_all(by_rows(green), "energy", 0, 0, tiled=True)
+    rows = to_rows(by_rows(green))
     rows, lower_here, upper, where = lax.optimization_barrier(
         (rows, dress_lower(green, link), dress_upper(green_above, link), where)
     )

time: 149 us -> 150 us (level)
  the two profiles are of different devices: /device:TPU:35 before, /device:TPU:179 now
where the time goes in v5:
time: 150 us; the launch traced here: 149 us
  waiting for transfers between devices  86.9 us (58%)
  starting transfers between devices  39.9 us (27%)
  Pallas kernels  10.9 us (7%)
  local copies, waits for them, and re-layouts  7.28 us (5%)
  matrix products  3.05 us (2%)
    ppermute x2, waiting for transfers between devices, along_slabs(): return lax.ppermute(block, 'slab', route)  82.8 us
    all_to_all x1, starting transfers between devices, home_and_across(): lax.all_to_all(both.reshape(2 * ENERGY, *rows.shape[1:]), BOTH, 0, 0, axi...  13 us
    all_to_all x1, starting transfers between devices, to_rows(): lax.all_to_all(blocks, BOTH, 0, 0, axis_index_groups=groups, tiled=True)  10.3 us
    ppermute x1, starting transfers between devices, on_chip(): return lax.ppermute(block, 'slab', [(s, s ^ 1) for s in range(SLABS)])  8.95 us
    ppermute x2, starting transfers between devices, along_slabs(): return lax.ppermute(block, 'slab', route)  7.74 us
    unnamed x12, local copies, waits for them, and re-layouts  3.25 us
  transfers between devices with their start and end apart: 5, of which 4 were waited for; matrix products, arithmetic and copies ran while one was open for 5% of the time, Pallas kernels for 7%

profile of v5, /device:TPU:179, one launch (start us, length us, event | category | flops | bytes accessed | tf_op | source)
XLA Modules:
  0.0 149.1 jit_solution(4922214133019870897)
XLA Ops:
  0.6 2.6 %collective-permute-start = (bf16[2,512,512]{2,1,0:T(8,128)(2,1)}, bf16[2,512,512]{2,1,0:T(8,128)(2,1)S(1)}, u32[]{:S(2)}, u32[]{:S(2)}) collective-permute-start(bf16[2,512,512]{2,1,0:T(8,128)(2,1)} %bitcast.32), channel_id=1, source_target_pairs={{1,0},{2,1},{3,2},{4,3},{5,4},{6,5},{7,6},{8,7},{9,8},{10,9},{11,1... | collective-permute-start | bytes 3145736 | tf_op jit(solution)/shard_map/ppermute | solution.py:28
  3.2 0.0 copy-start
  3.2 0.0 copy-start.2
  3.2 2.4 %copy.16 = bf16[2,32,16,512]{3,2,0,1:T(8,128)(2,1)} copy(bf16[2,32,16,512]{3,2,1,0:T(8,128)(2,1)} %bitcast.33) | data formatting | bytes 2097152 | tf_op jit(solution)/shard_map/reshape;squeeze | solution.py:57
  5.6 10.3 %all-to-all-start = ((bf16[32,2,16,512]{3,2,1,0:T(8,128)(2,1)}), bf16[32,2,16,512]{3,2,1,0:T(8,128)(2,1)}, u32[]{:S(2)}, u32[]{:S(2)}) async-start(bf16[32,2,16,512]{3,2,1,0:T(8,128)(2,1)} %bitcast.42), calls=%async_computation | async-start | bytes 2097152 | tf_op jit(solution)/shard_map/all_to_all | solution.py:183
  16.0 0.0 copy-done
  16.0 0.0 copy-done.2
  16.0 2.4 %shard_map.59 = bf16[2,512,512]{2,1,0:T(8,128)(2,1)} custom-call(bf16[2,512,512]{2,1,0:T(8,128)(2,1)S(1)} %bitcast.34, bf16[512,512]{1,0:T(8,128)(2,1)S(1)} %bitcast.36), custom_call_target="tpu_custom_call" | custom-call | flops 1073741824 | bytes 2621440 | tf_op jit(solution)/shard_map/pallas_call | solution.py:66
  18.4 0.1 pad_add_fusion.where_ref
  18.5 31.7 %collective-permute-done.g_ref = bf16[2,512,512]{2,1,0:T(8,128)(2,1)S(1)} collective-permute-done((bf16[2,512,512]{2,1,0:T(8,128)(2,1)}, bf16[2,512,512]{2,1,0:T(8,128)(2,1)S(1)}, u32[]{:S(2)}, u32[]{:S(2)}) %collective-permute-start) | collective-permute-done | bytes 1048608 | tf_op jit(solution)/shard_map/ppermute | solution.py:28
  50.1 0.0 copy-start.3
  50.1 1.0 copy-done.3
  51.2 1.6 %shard_map.60.b_ref = bf16[2,512,512]{2,1,0:T(8,128)(2,1)S(1)} custom-call(bf16[2,512,512]{2,1,0:T(8,128)(2,1)S(1)} %collective-permute-done.g_ref, bf16[512,512]{1,0:T(8,128)(2,1)S(1)} %bitcast.37), custom_call_target="tpu_custom_call" | custom-call | flops 134217728000 | bytes 2621440 | tf_op jit(solution)/shard_map/pallas_call | solution.py:89
  52.8 0.0 copy-start.4
  52.8 2.0 %all-to-all-done = bf16[32,2,16,512]{3,2,1,0:T(8,128)(2,1)} async-done(((bf16[32,2,16,512]{3,2,1,0:T(8,128)(2,1)}), bf16[32,2,16,512]{3,2,1,0:T(8,128)(2,1)}, u32[]{:S(2)}, u32[]{:S(2)}) %all-to-all-start) | async-done | bytes 1048608 | tf_op jit(solution)/shard_map/all_to_all | solution.py:183
  54.8 1.8 %copy.13 = bf16[8,8,16,512]{3,1,2,0:T(8,128)(2,1)S(1)} copy(bf16[8,8,16,512]{3,2,1,0:T(8,128)(2,1)} %bitcast.17) | data formatting | bytes 2097152
  56.7 5.2 %collective-permute-start.1 = (bf16[2,512,512]{2,1,0:T(8,128)(2,1)}, bf16[2,512,512]{2,1,0:T(8,128)(2,1)}, u32[]{:S(2)}, u32[]{:S(2)}) collective-permute-start(bf16[2,512,512]{2,1,0:T(8,128)(2,1)} %shard_map.59), channel_id=1, source_target_pairs={{0,1},{1,2},{2,3},{3,4},{4,5},{5,6},{6,7},{7,8},{8,9},{9,10},{10,1... | collective-permute-start | bytes 3145736 | tf_op jit(solution)/shard_map/ppermute | solution.py:28
  61.8 0.0 copy-done.4
  61.8 0.8 convolution_multiply_fusion
  62.7 1.0 fusion
  63.7 1.3 fusion.1
  64.9 0.4 copy.14
  65.3 0.2 pad_maximum_fusion
  65.5 1.6 %copy.10 = bf16[32,2,2,16,512]{4,3,2,1,0:T(8,128)(2,1)} copy(bf16[32,2,2,16,512]{4,3,2,0,1:T(8,128)(2,1)S(1)} %pad_maximum_fusion) | data formatting | bytes 4194304 | tf_op jit(solution)/shard_map/stack | solution.py:36
  67.0 13.0 %all-to-all-start.1 = ((bf16[64,2,16,512]{3,2,1,0:T(8,128)(2,1)}), bf16[64,2,16,512]{3,2,1,0:T(8,128)(2,1)S(1)}, u32[]{:S(2)}, u32[]{:S(2)}) async-start(bf16[64,2,16,512]{3,2,1,0:T(8,128)(2,1)} %bitcast.40), calls=%async_computation.1 | async-start | bytes 4194304 | tf_op jit(solution)/shard_map/all_to_all | solution.py:37
  80.0 51.1 %collective-permute-done.1.a_ref.arrived_ref = bf16[2,512,512]{2,1,0:T(8,128)(2,1)} collective-permute-done((bf16[2,512,512]{2,1,0:T(8,128)(2,1)}, bf16[2,512,512]{2,1,0:T(8,128)(2,1)}, u32[]{:S(2)}, u32[]{:S(2)}) %collective-permute-start.1) | collective-permute-done | bytes 1048608 | tf_op jit(solution)/shard_map/ppermute | solution.py:28
  131.1 1.1 shard_map.62.where
  132.3 2.1 %shard_map.61 = bf16[2,512,512]{2,1,0:T(8,128)(2,1)} custom-call(bf16[2,512,512]{2,1,0:T(8,128)(2,1)} %collective-permute-done.1.a_ref.arrived_ref, bf16[2,512,512]{2,1,0:T(8,128)(2,1)S(1)} %shard_map.60.b_ref), custom_call_target="tpu_custom_call" | custom-call | flops 524288 | bytes 3145728 | tf_op jit(solution)/shard_map/pallas_call | solution.py:106
  134.4 0.0 copy-start.1
  134.4 2.1 %all-to-all-done.1 = bf16[64,2,16,512]{3,2,1,0:T(8,128)(2,1)S(1)} async-done(((bf16[64,2,16,512]{3,2,1,0:T(8,128)(2,1)}), bf16[64,2,16,512]{3,2,1,0:T(8,128)(2,1)S(1)}, u32[]{:S(2)}, u32[]{:S(2)}) %all-to-all-start.1) | async-done | bytes 2097184 | tf_op jit(solution)/shard_map/all_to_all | solution.py:37
  136.5 0.1 dynamic-slice_bitcast_fusion
  136.6 8.9 %collective-permute-start.2 = (bf16[32,2,16,512]{3,2,1,0:T(8,128)(2,1)S(1)}, bf16[32,2,16,512]{3,2,1,0:T(8,128)(2,1)S(1)}, u32[]{:S(2)}, u32[]{:S(2)}) collective-permute-start(bf16[32,2,16,512]{3,2,1,0:T(8,128)(2,1)S(1)} %dynamic-slice_bitcast_fusion), channel_id=1, source_target_pairs={{0,1},{1,0},{2,3},{3,2},{4,5},{5,4},{6,7},{7,6},{8,9},{9,8},{10,11... | collective-permute-start | bytes 3145736 | tf_op jit(solution)/shard_map/ppermute | solution.py:49
  145.5 0.0 copy-done.1
  145.5 2.4 %shard_map.63.s_ref = f32[2,512,512]{2,1,0:T(8,128)S(1)} custom-call(s32[2]{0:T(128)S(1)} %shard_map.62.where, bf16[32,2,2,16,512]{4,3,2,1,0:T(8,128)(2,1)S(1)} %bitcast.30, bf16[32,2,2,16,512]{4,3,2,1,0:T(8,128)(2,1)S(1)} %bitcast.31, bf16[512,512]{1,0:T(8,128)(2,1)S(1)} %bitcast.35), custom_call_target="tpu_custom_call" | custom-call | flops 1073741824 | bytes 4718592 | tf_op jit(solution)/shard_map/pallas_call | solution.py:143
  147.9 0.0 collective-permute-done.2.p_ref
  147.9 1.2 shard_map.64
Async XLA Ops:
  0.6 49.5 %collective-permute-start = (bf16[2,512,512]{2,1,0:T(8,128)(2,1)}, bf16[2,512,512]{2,1,0:T(8,128)(2,1)S(1)}, u32[]{:S(2)}, u32[]{:S(2)}) collective-permute-start(bf16[2,512,512]{2,1,0:T(8,128)(2,1)} %bitcast.32), channel_id=1, source_target_pairs={{1,0},{2,1},{3,2},{4,3},{5,4},{6,5},{7,6},{8,7},{9,8},{10,9},{11,1... | collective-permute-start | bytes 3145736 | tf_op jit(solution)/shard_map/ppermute | solution.py:28
  3.2 12.7 %copy-start = (bf16[2,1,512,512]{3,2,1,0:T(8,128)(2,1)S(1)}, bf16[2,1,512,512]{3,2,1,0:T(8,128)(2,1)}, u32[]{:S(2)}) copy-start(bf16[2,1,512,512]{3,2,1,0:T(8,128)(2,1)} %param.4) | copy-start | bytes 3145732
  3.2 12.7 %copy-start.2 = (bf16[1,512,512]{2,1,0:T(8,128)(2,1)S(1)}, bf16[1,512,512]{2,1,0:T(8,128)(2,1)}, u32[]{:S(2)}) copy-start(bf16[1,512,512]{2,1,0:T(8,128)(2,1)} %param.5) | copy-start | bytes 1572868
  5.6 49.2 %all-to-all-start = ((bf16[32,2,16,512]{3,2,1,0:T(8,128)(2,1)}), bf16[32,2,16,512]{3,2,1,0:T(8,128)(2,1)}, u32[]{:S(2)}, u32[]{:S(2)}) async-start(bf16[32,2,16,512]{3,2,1,0:T(8,128)(2,1)} %bitcast.42), calls=%async_computation | async-start | bytes 2097152 | tf_op jit(solution)/shard_map/all_to_all | solution.py:183
  50.1 1.0 copy-start.3
  52.8 9.0 %copy-start.4 = (s32[64]{0:T(128)S(1)}, s32[64]{0:T(128)}, u32[]{:S(2)}) copy-start(s32[64]{0:T(128)} %constant.36.clone) | copy-start | bytes 772
  56.7 74.4 %collective-permute-start.1 = (bf16[2,512,512]{2,1,0:T(8,128)(2,1)}, bf16[2,512,512]{2,1,0:T(8,128)(2,1)}, u32[]{:S(2)}, u32[]{:S(2)}) collective-permute-start(bf16[2,512,512]{2,1,0:T(8,128)(2,1)} %shard_map.59), channel_id=1, source_target_pairs={{0,1},{1,2},{2,3},{3,4},{4,5},{5,6},{6,7},{7,8},{8,9},{9,10},{10,1... | collective-permute-start | bytes 3145736 | tf_op jit(solution)/shard_map/ppermute | solution.py:28
  67.0 69.5 %all-to-all-start.1 = ((bf16[64,2,16,512]{3,2,1,0:T(8,128)(2,1)}), bf16[64,2,16,512]{3,2,1,0:T(8,128)(2,1)S(1)}, u32[]{:S(2)}, u32[]{:S(2)}) async-start(bf16[64,2,16,512]{3,2,1,0:T(8,128)(2,1)} %bitcast.40), calls=%async_computation.1 | async-start | bytes 4194304 | tf_op jit(solution)/shard_map/all_to_all | solution.py:37
  134.4 11.1 %copy-start.1 = (bf16[1,512,512]{2,1,0:T(8,128)(2,1)S(1)}, bf16[1,512,512]{2,1,0:T(8,128)(2,1)}, u32[]{:S(2)}) copy-start(bf16[1,512,512]{2,1,0:T(8,128)(2,1)} %param.6) | copy-start | bytes 1572868
  136.6 11.4 %collective-permute-start.2 = (bf16[32,2,16,512]{3,2,1,0:T(8,128)(2,1)S(1)}, bf16[32,2,16,512]{3,2,1,0:T(8,128)(2,1)S(1)}, u32[]{:S(2)}, u32[]{:S(2)}) collective-permute-start(bf16[32,2,16,512]{3,2,1,0:T(8,128)(2,1)S(1)} %dynamic-slice_bitcast_fusion), channel_id=1, source_target_pairs={{0,1},{1,0},{2,3},{3,2},{4,5},{5,4},{6,7},{7,6},{8,9},{9,8},{10,11... | collective-permute-start | bytes 3145736 | tf_op jit(solution)/shard_map/ppermute | solution.py:49
